TPU v7x, 512 devices: a whole 4x4x16 slice. The times are simulated.
512 devices in a mesh: member: 32 (over y, z_lo, core), region: 16 (over z_hi, x).
Axes of the slice: x: 4, y: 4, z: 16 (z_hi: 4, z_lo: 4; z = z_hi * 4 + z_lo), core: 2. Of those that a mesh axis runs over, the one named last changes fastest.
Arguments:
- ensemble: float32 [256, 76, 8192], P('member', None, 'region'), may hold values from -6 to 6
- blending_matrix: float32 [76, 76], replicated, may hold values from -0.625 to 0.625
- lateral_spreading: float32 [76], replicated, may hold values from 0.19 to 0.2
- obs_op: float32 [1024, 128, 608], P(('region', 'member')), may hold values from -0.25 to 0.25
- obs_value: float32 [1024, 128], P(('region', 'member')), may hold values from -6 to 6
- obs_precision: float32 [1024, 128], P(('region', 'member')), may hold values from 0.01 to 3000
Outputs:
- analysis: float32 [256, 76, 8192], P('member', None, 'region')
All inputs are finite; a program needn't handle non-finite values.
Results may differ from a plain program's by a relative error of at most 0.0003.
Values sent between devices are 32-bit elements; how exact they have to be, the bound alone decides.
No kernel may reach another device: no remote copies, remote signals or barrier semaphores. Data moves between devices by JAX's collectives and lax.ppermute only.
A program may use at most 64 MiB of HBM per device.

v0:
```python
import math

import jax
import jax.numpy as jnp
from jax import lax
from jax.sharding import PartitionSpec as P

GY = 128
NSTEP = 4
ITERS = 12


HIGHEST = lax.Precision.HIGHEST


def extended(cells, sides, width):
    for axis, dim in sides:
        count = lax.axis_size(axis)
        head = lax.slice_in_dim(cells, 0, width, axis=dim)
        tail = lax.slice_in_dim(cells, cells.shape[dim] - width, cells.shape[dim], axis=dim)
        cells = jnp.concatenate(
            [
                lax.ppermute(tail, axis, [(i, (i + 1) % count) for i in range(count)]),
                cells,
                lax.ppermute(head, axis, [((i + 1) % count, i) for i in range(count)]),
            ],
            axis=dim,
        )
    return cells


def analyse(packed):
    patch_state, operator, observed, precisions = packed
    ens_size = patch_state.shape[0]
    mean_state = jnp.mean(patch_state, axis=0)
    perturb = patch_state - mean_state
    obs_pert = jnp.dot(perturb, operator.T, precision=HIGHEST, preferred_element_type=jnp.float32)
    obs_mean = jnp.dot(operator, mean_state, precision=HIGHEST, preferred_element_type=jnp.float32)
    innovation = observed - obs_mean
    weighted = obs_pert * precisions
    gram_matrix = jnp.dot(
        weighted, obs_pert.T, precision=HIGHEST, preferred_element_type=jnp.float32
    )
    identity = jnp.eye(ens_size, dtype=jnp.float32)
    system = (ens_size - 1.0) * identity + gram_matrix
    norm_scale = jnp.sqrt(jnp.sum(system * system))
    sqrt_iter = system / norm_scale
    inv_iter = identity
    for step_index in range(ITERS):
        factor = 0.5 * (
            3.0 * identity
            - jnp.dot(inv_iter, sqrt_iter, precision=HIGHEST, preferred_element_type=jnp.float32)
        )
        sqrt_iter = jnp.dot(
            sqrt_iter, factor, precision=HIGHEST, preferred_element_type=jnp.float32
        )
        inv_iter = jnp.dot(factor, inv_iter, precision=HIGHEST, preferred_element_type=jnp.float32)
    inv_sqrt = inv_iter / jnp.sqrt(norm_scale)
    inverse = jnp.dot(inv_sqrt, inv_sqrt, precision=HIGHEST, preferred_element_type=jnp.float32)
    mean_w = jnp.dot(
        inverse,
        jnp.dot(weighted, innovation, precision=HIGHEST, preferred_element_type=jnp.float32),
        precision=HIGHEST,
        preferred_element_type=jnp.float32,
    )
    weights = math.sqrt(ens_size - 1.0) * inv_sqrt + mean_w[:, None]
    return mean_state + jnp.dot(
        weights.T, perturb, precision=HIGHEST, preferred_element_type=jnp.float32
    )


def shards(ensemble, blending_matrix, lateral_spreading, obs_op, obs_value, obs_precision):
    mem_dev, levels, cols_dev = ensemble.shape
    row_count = cols_dev // GY
    layered_variables = ensemble.reshape(mem_dev, levels, row_count, GY)
    diffuse_rate = lateral_spreading[None, :, None, None]
    for step_index in range(NSTEP):
        padded = extended(layered_variables, (("region", 2),), 1)
        centre = padded[:, :, 1:-1, :]
        laplace = (
            padded[:, :, 2:, :]
            + padded[:, :, :-2, :]
            + jnp.roll(centre, -1, 3)
            + jnp.roll(centre, 1, 3)
            - 4.0 * centre
        )
        coupled = jnp.einsum("fg,mgxy->mfxy", blending_matrix, centre, precision=HIGHEST)
        layered_variables = centre + diffuse_rate * laplace + 0.3 * jnp.tanh(coupled)
    members = lax.axis_size("member")
    patch_count = obs_op.shape[0]
    patch_cols = cols_dev // (members * patch_count)
    entry_width = mem_dev * levels * patch_cols
    split_cols = layered_variables.reshape(mem_dev, levels, members, patch_count, patch_cols)
    outgoing = split_cols.transpose(2, 3, 0, 1, 4).reshape(members, patch_count, entry_width)
    at_owner = lax.all_to_all(outgoing, "member", split_axis=0, concat_axis=2, tiled=True)
    ens_total = mem_dev * members
    neighbourhood_tiles = at_owner.reshape(patch_count, ens_total, levels * patch_cols)
    result = lax.map(analyse, (neighbourhood_tiles, obs_op, obs_value, obs_precision))
    backward = result.reshape(patch_count, members, entry_width)
    returned = lax.all_to_all(backward, "member", split_axis=1, concat_axis=0, tiled=True)
    restored = returned.reshape(members, patch_count, mem_dev, levels, patch_cols).transpose(
        2, 3, 0, 1, 4
    )
    return restored.reshape(mem_dev, levels, cols_dev)


def solution(mesh):
    return jax.shard_map(
        shards,
        mesh=mesh,
        in_specs=(
            P("member", None, "region"),
            P(),
            P(),
            P(("region", "member"), None, None),
            P(("region", "member"), None),
            P(("region", "member"), None),
        ),
        out_specs=P("member", None, "region"),
        check_vma=False,
    )
```

profile of v0, /device:TPU:1, one launch (start us, length us, event | category | flops | bytes accessed | tf_op | source)
XLA Modules:
  0.0 310.4 jit_solution(8858619034460949602)
XLA Ops:
  2.1 15.5 %collective-permute-start = (f32[8,76,1,128]{3,1,2,0:T(8,128)S(1)}, f32[8,76,1,128]{3,1,2,0:T(8,128)S(1)}, u32[]{:S(2)}, u32[]{:S(2)}) collective-permute-start(f32[8,76,1,128]{3,1,2,0:T(8,128)S(1)} %get-tuple-element.86), channel_id=1, source_target_pairs={{1,0},{2,1},{3,2},{4,3},{5,4},{6,5},{7,6},{8,7},{9,8},{10,9},{11,1... | collective-permute-start | bytes 933896 | tf_op jit(solution)/shard_map/ppermute | solution.py:25
  20.4 25.2 %collective-permute-done = f32[8,76,1,128]{3,1,2,0:T(8,128)S(1)} collective-permute-done((f32[8,76,1,128]{3,1,2,0:T(8,128)S(1)}, f32[8,76,1,128]{3,1,2,0:T(8,128)S(1)}, u32[]{:S(2)}, u32[]{:S(2)}) %collective-permute-start) | collective-permute-done | bytes 311328 | tf_op jit(solution)/shard_map/ppermute | solution.py:25
  45.6 9.4 %collective-permute-done.1 = f32[8,76,1,128]{3,1,2,0:T(8,128)S(1)} collective-permute-done((f32[8,76,1,128]{3,1,2,0:T(8,128)S(1)}, f32[8,76,1,128]{3,1,2,0:T(8,128)S(1)}, u32[]{:S(2)}, u32[]{:S(2)}) %collective-permute-start.1) | collective-permute-done | bytes 311328 | tf_op jit(solution)/shard_map/ppermute | solution.py:23
  55.0 2.1 fusion.48
  59.5 3.4 %collective-permute-start.3 = (f32[8,76,1,128]{3,1,2,0:T(8,128)S(1)}, f32[8,76,1,128]{3,1,2,0:T(8,128)S(1)}, u32[]{:S(2)}, u32[]{:S(2)}) collective-permute-start(f32[8,76,1,128]{3,1,2,0:T(8,128)S(1)} %get-tuple-element.81), channel_id=1, source_target_pairs={{0,1},{1,2},{2,3},{3,4},{4,5},{5,6},{6,7},{7,8},{8,9},{9,10},{10,1... | collective-permute-start | bytes 933896 | tf_op jit(solution)/shard_map/ppermute | solution.py:23
  63.4 6.9 %collective-permute-done.2 = f32[8,76,1,128]{3,1,2,0:T(8,128)S(1)} collective-permute-done((f32[8,76,1,128]{3,1,2,0:T(8,128)S(1)}, f32[8,76,1,128]{3,1,2,0:T(8,128)S(1)}, u32[]{:S(2)}, u32[]{:S(2)}) %collective-permute-start.2) | collective-permute-done | bytes 311328 | tf_op jit(solution)/shard_map/ppermute | solution.py:25
  70.3 20.8 %collective-permute-done.3 = f32[8,76,1,128]{3,1,2,0:T(8,128)S(1)} collective-permute-done((f32[8,76,1,128]{3,1,2,0:T(8,128)S(1)}, f32[8,76,1,128]{3,1,2,0:T(8,128)S(1)}, u32[]{:S(2)}, u32[]{:S(2)}) %collective-permute-start.3) | collective-permute-done | bytes 311328 | tf_op jit(solution)/shard_map/ppermute | solution.py:23
  91.1 2.1 fusion.50
  95.7 3.4 %collective-permute-start.5 = (f32[8,76,1,128]{3,1,2,0:T(8,128)S(1)}, f32[8,76,1,128]{3,1,2,0:T(8,128)S(1)}, u32[]{:S(2)}, u32[]{:S(2)}) collective-permute-start(f32[8,76,1,128]{3,1,2,0:T(8,128)S(1)} %get-tuple-element.75), channel_id=1, source_target_pairs={{0,1},{1,2},{2,3},{3,4},{4,5},{5,6},{6,7},{7,8},{8,9},{9,10},{10,1... | collective-permute-start | bytes 933896 | tf_op jit(solution)/shard_map/ppermute | solution.py:23
  99.5 23.4 %collective-permute-done.4 = f32[8,76,1,128]{3,1,2,0:T(8,128)S(1)} collective-permute-done((f32[8,76,1,128]{3,1,2,0:T(8,128)S(1)}, f32[8,76,1,128]{3,1,2,0:T(8,128)S(1)}, u32[]{:S(2)}, u32[]{:S(2)}) %collective-permute-start.4) | collective-permute-done | bytes 311328 | tf_op jit(solution)/shard_map/ppermute | solution.py:25
  122.9 2.1 fusion.52
  125.5 10.1 %collective-permute-start.6 = (f32[8,76,1,128]{3,1,2,0:T(8,128)S(1)}, f32[8,76,1,128]{3,1,2,0:T(8,128)S(1)}, u32[]{:S(2)}, u32[]{:S(2)}) collective-permute-start(f32[8,76,1,128]{3,1,2,0:T(8,128)S(1)} %get-tuple-element.68), channel_id=1, source_target_pairs={{1,0},{2,1},{3,2},{4,3},{5,4},{6,5},{7,6},{8,7},{9,8},{10,9},{11,1... | collective-permute-start | bytes 933896 | tf_op jit(solution)/shard_map/ppermute | solution.py:25
  135.6 2.1 collective-permute-start.7
  138.2 18.0 %collective-permute-done.6 = f32[8,76,1,128]{3,1,2,0:T(8,128)S(1)} collective-permute-done((f32[8,76,1,128]{3,1,2,0:T(8,128)S(1)}, f32[8,76,1,128]{3,1,2,0:T(8,128)S(1)}, u32[]{:S(2)}, u32[]{:S(2)}) %collective-permute-start.6) | collective-permute-done | bytes 311328 | tf_op jit(solution)/shard_map/ppermute | solution.py:25
  156.2 2.1 fusion.54
  159.2 3.8 %copy.38 = f32[32,2,8,76,8]{0,4,3,2,1:T(8,128)} copy(f32[32,2,8,76,8]{3,4,1,0,2:T(8,128)S(1)} %bitcast.325) | data formatting | bytes 2490368 | tf_op jit(solution)/shard_map/transpose | solution.py:94
  163.0 5.0 %copy.39 = f32[32,2,4864]{2,1,0:T(2,128)} copy(f32[32,2,4864]{0,2,1:T(8,128)} %bitcast.322) | data formatting | bytes 2490368 | tf_op jit(solution)/shard_map/reshape | solution.py:94
  167.9 18.2 %all-to-all-start = ((f32[32,2,4864]{2,1,0:T(2,128)}), f32[32,2,4864]{2,1,0:T(2,128)S(1)}, u32[]{:S(2)}, u32[]{:S(2)}) async-start(f32[32,2,4864]{2,1,0:T(2,128)} %copy.39), calls=%async_computation | async-start | bytes 2490368 | tf_op jit(solution)/shard_map/all_to_all | solution.py:95
  186.1 32.0 %all-to-all-done = f32[32,2,4864]{2,1,0:T(2,128)S(1)} async-done(((f32[32,2,4864]{2,1,0:T(2,128)}), f32[32,2,4864]{2,1,0:T(2,128)S(1)}, u32[]{:S(2)}, u32[]{:S(2)}) %all-to-all-start) | async-done | bytes 1245216 | tf_op jit(solution)/shard_map/all_to_all | solution.py:95
  219.3 2.3 reshape.38
  222.7 39.0 %while.10 = (s32[]{:T(128)}, f32[2,256,608]{1,2,0:T(8,128)}, f32[2,256,608]{1,2,0:T(8,128)S(1)}, f32[2,128,608]{1,2,0:T(8,128)S(1)}, f32[2,128]{1,0:T(2,128)S(1)}, /*index=5*/f32[2,128]{1,0:T(2,128)S(1)}, s32[]{:T(128)}) while((s32[]{:T(128)}, f32[2,256,608]{1,2,0:T(8,128)}, f32[2,256,608]{1,2,0:T(8,128)S(1)}, f32[2,128,608]{1,2,0:T(8,128)S(1)}, ...), condition=%wide.region_3.4_spmd, body=%wide.region_0.3_spmd.sunk | while | flops 8072380416 | bytes 31855604 | solution.py:98
  264.8 36.1 %all_to_all.30 = f32[2,32,4864]{2,0,1:T(2,128)S(1)} all-to-all(f32[2,32,4864]{2,0,1:T(2,128)S(1)} %copy.43), channel_id=1, replica_groups=mesh['member'=32,'region'=16] {'member'}, dimensions={1} | all-to-all | bytes 2490368 | tf_op jit(solution)/shard_map/all_to_all | solution.py:100
  300.9 3.5 %copy.44 = f32[32,2,1,4864]{0,3,1,2:T(8,128)} copy(f32[32,2,1,4864]{3,1,0,2:T(2,128)S(1)} %bitcast.327) | data formatting | bytes 2490368 | tf_op jit(solution)/shard_map/all_to_all | solution.py:100
  304.3 4.3 %copy.45 = f32[8,76,32,2,8]{1,4,3,2,0:T(8,128)S(1)} copy(f32[8,76,32,2,8]{2,4,1,0,3:T(8,128)} %bitcast.323) | data formatting | bytes 2490368 | tf_op jit(solution)/shard_map/transpose | solution.py:101
  (130 shorter events, 56.2 us)
Async XLA Ops:
  0.0 55.0 %copy-start = (f32[76,76]{1,0:T(8,128)S(1)}, f32[76,76]{1,0:T(8,128)}, u32[]{:S(2)}) copy-start(f32[76,76]{1,0:T(8,128)} %param.9) | copy-start | bytes 69316
  2.1 43.5 %collective-permute-start = (f32[8,76,1,128]{3,1,2,0:T(8,128)S(1)}, f32[8,76,1,128]{3,1,2,0:T(8,128)S(1)}, u32[]{:S(2)}, u32[]{:S(2)}) collective-permute-start(f32[8,76,1,128]{3,1,2,0:T(8,128)S(1)} %get-tuple-element.86), channel_id=1, source_target_pairs={{1,0},{2,1},{3,2},{4,3},{5,4},{6,5},{7,6},{8,7},{9,8},{10,9},{11,1... | collective-permute-start | bytes 933896 | tf_op jit(solution)/shard_map/ppermute | solution.py:25
  17.6 37.4 %collective-permute-start.1 = (f32[8,76,1,128]{3,1,2,0:T(8,128)S(1)}, f32[8,76,1,128]{3,1,2,0:T(8,128)S(1)}, u32[]{:S(2)}, u32[]{:S(2)}) collective-permute-start(f32[8,76,1,128]{3,1,2,0:T(8,128)S(1)} %get-tuple-element.87), channel_id=1, source_target_pairs={{0,1},{1,2},{2,3},{3,4},{4,5},{5,6},{6,7},{7,8},{8,9},{9,10},{10,1... | collective-permute-start | bytes 933896 | tf_op jit(solution)/shard_map/ppermute | solution.py:23
  19.9 35.0 %copy-start.3 = (f32[76]{0:T(128)S(1)}, f32[76]{0:T(128)}, u32[]{:S(2)}) copy-start(f32[76]{0:T(128)} %param.10) | copy-start | bytes 916
  57.6 12.7 %collective-permute-start.2 = (f32[8,76,1,128]{3,1,2,0:T(8,128)S(1)}, f32[8,76,1,128]{3,1,2,0:T(8,128)S(1)}, u32[]{:S(2)}, u32[]{:S(2)}) collective-permute-start(f32[8,76,1,128]{3,1,2,0:T(8,128)S(1)} %get-tuple-element.80), channel_id=1, source_target_pairs={{1,0},{2,1},{3,2},{4,3},{5,4},{6,5},{7,6},{8,7},{9,8},{10,9},{11,1... | collective-permute-start | bytes 933896 | tf_op jit(solution)/shard_map/ppermute | solution.py:25
  59.5 31.5 %collective-permute-start.3 = (f32[8,76,1,128]{3,1,2,0:T(8,128)S(1)}, f32[8,76,1,128]{3,1,2,0:T(8,128)S(1)}, u32[]{:S(2)}, u32[]{:S(2)}) collective-permute-start(f32[8,76,1,128]{3,1,2,0:T(8,128)S(1)} %get-tuple-element.81), channel_id=1, source_target_pairs={{0,1},{1,2},{2,3},{3,4},{4,5},{5,6},{6,7},{7,8},{8,9},{9,10},{10,1... | collective-permute-start | bytes 933896 | tf_op jit(solution)/shard_map/ppermute | solution.py:23
  93.7 29.1 %collective-permute-start.4 = (f32[8,76,1,128]{3,1,2,0:T(8,128)S(1)}, f32[8,76,1,128]{3,1,2,0:T(8,128)S(1)}, u32[]{:S(2)}, u32[]{:S(2)}) collective-permute-start(f32[8,76,1,128]{3,1,2,0:T(8,128)S(1)} %get-tuple-element.74), channel_id=1, source_target_pairs={{1,0},{2,1},{3,2},{4,3},{5,4},{6,5},{7,6},{8,7},{9,8},{10,9},{11,1... | collective-permute-start | bytes 933896 | tf_op jit(solution)/shard_map/ppermute | solution.py:25
  95.7 27.2 %collective-permute-start.5 = (f32[8,76,1,128]{3,1,2,0:T(8,128)S(1)}, f32[8,76,1,128]{3,1,2,0:T(8,128)S(1)}, u32[]{:S(2)}, u32[]{:S(2)}) collective-permute-start(f32[8,76,1,128]{3,1,2,0:T(8,128)S(1)} %get-tuple-element.75), channel_id=1, source_target_pairs={{0,1},{1,2},{2,3},{3,4},{4,5},{5,6},{6,7},{7,8},{8,9},{9,10},{10,1... | collective-permute-start | bytes 933896 | tf_op jit(solution)/shard_map/ppermute | solution.py:23
  125.5 30.7 %collective-permute-start.6 = (f32[8,76,1,128]{3,1,2,0:T(8,128)S(1)}, f32[8,76,1,128]{3,1,2,0:T(8,128)S(1)}, u32[]{:S(2)}, u32[]{:S(2)}) collective-permute-start(f32[8,76,1,128]{3,1,2,0:T(8,128)S(1)} %get-tuple-element.68), channel_id=1, source_target_pairs={{1,0},{2,1},{3,2},{4,3},{5,4},{6,5},{7,6},{8,7},{9,8},{10,9},{11,1... | collective-permute-start | bytes 933896 | tf_op jit(solution)/shard_map/ppermute | solution.py:25
  135.6 20.5 %collective-permute-start.7 = (f32[8,76,1,128]{3,1,2,0:T(8,128)S(1)}, f32[8,76,1,128]{3,1,2,0:T(8,128)S(1)}, u32[]{:S(2)}, u32[]{:S(2)}) collective-permute-start(f32[8,76,1,128]{3,1,2,0:T(8,128)S(1)} %get-tuple-element.69), channel_id=1, source_target_pairs={{0,1},{1,2},{2,3},{3,4},{4,5},{5,6},{6,7},{7,8},{8,9},{9,10},{10,1... | collective-permute-start | bytes 933896 | tf_op jit(solution)/shard_map/ppermute | solution.py:23
  167.9 50.2 %all-to-all-start = ((f32[32,2,4864]{2,1,0:T(2,128)}), f32[32,2,4864]{2,1,0:T(2,128)S(1)}, u32[]{:S(2)}, u32[]{:S(2)}) async-start(f32[32,2,4864]{2,1,0:T(2,128)} %copy.39), calls=%async_computation | async-start | bytes 2490368 | tf_op jit(solution)/shard_map/all_to_all | solution.py:95
  221.6 1.1 copy-start.2
  221.6 1.1 copy-start.4
  221.7 1.1 copy-start.5
  308.6 1.8 copy-start.1
where the time goes:
time: 311 us; the launch traced here: 310 us
  waiting for transfers between devices  136 us (44%)
  starting transfers between devices  58.4 us (19%)
  matrix products  45.1 us (15%)
  blocking collectives  36.1 us (12%)
  local copies, waits for them, and re-layouts  32.3 us (10%)
    ppermute x4, waiting for transfers between devices, extended(): lax.ppermute(head, axis, [((i + 1) % count, i) for i in range(count)])  73.5 us
    all_to_all x1, blocking collectives, shards(): lax.all_to_all(backward, 'member', split_axis=1, concat_axis=0, tiled=True)  36.1 us
    all_to_all x1, waiting for transfers between devices, shards(): lax.all_to_all(outgoing, 'member', split_axis=0, concat_axis=2, tiled=True)  32 us
    ppermute x4, waiting for transfers between devices, extended(): lax.ppermute(tail, axis, [(i, (i + 1) % count) for i in range(count)])  30.2 us
    ppermute x4, starting transfers between devices, extended(): lax.ppermute(head, axis, [((i + 1) % count, i) for i in range(count)])  29.4 us
    all_to_all x1, starting transfers between devices, shards(): lax.all_to_all(outgoing, 'member', split_axis=0, concat_axis=2, tiled=True)  18.2 us
    ppermute x4, starting transfers between devices, extended(): lax.ppermute(tail, axis, [(i, (i + 1) % count) for i in range(count)])  10.7 us
    dot_general x24, matrix products, analyse(): jnp.dot(inv_iter, sqrt_iter, precision=HIGHEST, preferred_element_type=jn...  9.01 us
  transfers between devices with their start and end apart: 9, of which 7 were waited for; matrix products, arithmetic and copies ran while one was open for 1% of the time, Pallas kernels for 0%

commit v1 on v0

v1 whole, which is shorter than its diff:
```python
import math

import jax
import jax.numpy as jnp
from jax import lax
from jax.experimental import pallas as pl
from jax.experimental.pallas import tpu as pltpu
from jax.sharding import Mesh, PartitionSpec as P

F32 = jnp.float32
BF16 = jnp.bfloat16
HIGHEST = lax.Precision.HIGHEST
LEVELS = 76
PADDED = 80
GY = 128
NSTEP = 4
ITERS = 12
MEMBERS = 256
PAIR = 2 * LEVELS * 16
TILES = PAIR // 128
HALF = LEVELS * 16
LANES = 1280
VMEM_LIMIT = 32 * 1024 * 1024


def lane_index(shape):
    return lax.broadcasted_iota(jnp.int32, shape, len(shape) - 1)


def split3(x):
    high = x.astype(BF16)
    rest = x - high.astype(F32)
    mid = rest.astype(BF16)
    low = (rest - mid.astype(F32)).astype(BF16)
    return high, mid, low


def swap_blocks(x):
    sub = lax.broadcasted_iota(jnp.int32, x.shape, 1)
    block = lane_index(x.shape) // 16
    for bit in (1, 2, 4):
        up = (sub & bit) != 0
        keep = up == ((block & bit) != 0)
        lanes = 16 * bit
        lower = pltpu.roll(pltpu.roll(x, 8 - bit, 1), lanes, 2)
        if bit == 4:
            other = lower
        else:
            upper = pltpu.roll(pltpu.roll(x, bit, 1), 128 - lanes, 2)
            other = jnp.where(up, upper, lower)
        x = jnp.where(keep, x, other)
    return x


def forecast_kernel(main_ref, prev_ref, next_ref, mix_ref, rate_ref, out_ref, state, mix, rate):
    wide = mix_ref[...]
    high, mid, low = split3(wide)
    part = lane_index(wide.shape) // PADDED
    pick_mid = (part == 2) | (part == 3)
    mix[...] = jnp.where(
        pick_mid, mid.astype(F32), jnp.where(part == 5, low.astype(F32), high.astype(F32))
    ).astype(BF16)
    rate[...] = jnp.broadcast_to(rate_ref[...], (PADDED, GY))
    pad = jnp.zeros((PADDED - LEVELS, GY), F32)
    for m in range(2):
        for row in range(24):
            cols = pl.ds((row % 4) * GY, GY)
            if row < 4:
                cells = prev_ref[m, :, cols]
            elif row < 20:
                cells = main_ref[row // 4 - 1, m, :, cols]
            else:
                cells = next_ref[m, :, cols]
            state[0, m, row, 0:LEVELS, :] = cells
            state[0, m, row, LEVELS:PADDED, :] = pad

    def advance(now, m, row):
        centre = [state[now, m, row + i] for i in range(2)]
        before = state[now, m, row - 1]
        after = state[now, m, row + 2]
        parts = split3(jnp.concatenate(centre, axis=1))
        stacked = jnp.concatenate([parts[i] for i in (0, 1, 0, 1, 2, 0)], axis=0)
        coupled = jnp.dot(mix[...], stacked, preferred_element_type=F32)
        result = []
        for i in range(2):
            cells = centre[i]
            around = (centre[1] + before) if i == 0 else (after + centre[0])
            laplace = (
                around + pltpu.roll(cells, GY - 1, 1) + pltpu.roll(cells, 1, 1) - 4.0 * cells
            )
            pushed = jnp.tanh(coupled[:, i * GY : (i + 1) * GY])
            result.append(cells + rate[...] * laplace + 0.3 * pushed)
        return result

    for step in range(NSTEP - 1):
        now = step % 2

        def body(pair, carry, now=now, step=step):
            row = step + 1 + 2 * pair
            for m in range(2):
                result = advance(now, m, row)
                state[1 - now, m, row] = result[0]
                state[1 - now, m, row + 1] = result[1]
            return carry

        lax.fori_loop(0, (22 - 2 * step) // 2, body, 0)

    def last(pair, carry):
        row = 4 + 2 * pair
        results = [advance((NSTEP - 1) % 2, m, row) for m in range(2)]
        for i in range(2):
            both = jnp.concatenate([results[m][i][0:LEVELS] for m in range(2)], axis=0)
            moved = swap_blocks(both.reshape(TILES, 8, GY))
            start = (2 * pair + i) * 8
            for tile in range(TILES):
                out_ref[pl.ds(start, 8), 0, pl.ds(tile * 128, 128)] = moved[tile]
        return carry

    lax.fori_loop(0, 8, last, 0)


def analysis_kernel(x_ref, op_ref, obs_ref, prec_ref, out_ref, pert, wide, yref, rr, zz, ff, moved):
    low_half = lane_index((128, 128)) < 64
    rows = 128
    for tile in range(10):
        even = x_ref[:, 0, pl.ds(tile * 128, 128)]
        first = x_ref[:, 0, pl.ds((9 + tile) * 128, 128)]
        if tile < 9:
            second = x_ref[:, 0, pl.ds((10 + tile) * 128, 128)]
            odd = pltpu.roll(jnp.where(low_half, second, first), 64, 1)
        else:
            even = jnp.where(low_half, even, 0.0)
            odd = jnp.where(low_half, pltpu.roll(first, 64, 1), 0.0)
        mean = (jnp.sum(even, axis=0, keepdims=True) + jnp.sum(odd, axis=0, keepdims=True)) / MEMBERS
        lanes = pl.ds(tile * 128, 128)
        pert[0:rows, lanes] = even - mean
        pert[rows : 2 * rows, lanes] = odd - mean
        pert[2 * rows : 2 * rows + 8, lanes] = jnp.broadcast_to(mean, (8, 128))

    take = lax.broadcasted_iota(jnp.int32, (128, 256), 0)
    put = lane_index((128, 256))
    same = (put // 16 == take // 8) & (put % 8 == take % 8)
    spread = jnp.where(same, 1.0, 0.0).astype(BF16)
    group = (lane_index((128, 256)) // 8) % 2
    for j in range(2):
        for block in range(5):
            width = 128 if block < 4 else 608 - 512
            piece = split3(op_ref[j, :, pl.ds(block * 128, width)])
            grown = [
                jnp.dot(p, spread[0:width], preferred_element_type=F32) for p in piece
            ]
            full = (grown[0] + grown[1]) + grown[2]
            wide[j * 128 : (j + 1) * 128, block * 256 : (block + 1) * 256] = jnp.where(
                group == j, full, 0.0
            )

    yref[...] = lax.dot_general(
        pert[...], wide[...], (((1,), (1,)), ((), ())), precision=HIGHEST, preferred_element_type=F32
    )
    eye = jnp.where(
        lax.broadcasted_iota(jnp.int32, (MEMBERS, MEMBERS), 0) == lane_index((MEMBERS, MEMBERS)), 1.0, 0.0
    )

    def mm(a, b):
        return jnp.dot(a, b, precision=HIGHEST, preferred_element_type=F32)

    scale = []
    for j in range(2):
        obs = slice(j * 128, (j + 1) * 128)
        y = yref[0:MEMBERS, obs]
        weighted = y * prec_ref[j : j + 1, :]
        gram = lax.dot_general(
            weighted, y, (((1,), (1,)), ((), ())), precision=HIGHEST, preferred_element_type=F32
        )
        system = (MEMBERS - 1.0) * eye + gram
        norm = jnp.sqrt(jnp.sum(jnp.sum(system * system, axis=0, keepdims=True), axis=1, keepdims=True))
        scale.append(norm)
        start = system / norm
        factor = 0.5 * (3.0 * eye - start)
        ff[j] = start
        zz[j] = factor
        rr[j] = mm(start, factor)

    def body(step, carry):
        for j in range(2):
            ff[j] = 0.5 * (3.0 * eye - mm(zz[j], rr[j]))
        for j in range(2):
            rr[j] = mm(rr[j], ff[j])
        for j in range(2):
            zz[j] = mm(ff[j], zz[j])
        return carry

    lax.fori_loop(0, ITERS - 2, body, 0)
    shifts = []
    for j in range(2):
        factor = 0.5 * (3.0 * eye - mm(zz[j], rr[j]))
        root = mm(factor, zz[j]) / jnp.sqrt(scale[j])
        obs = slice(j * 128, (j + 1) * 128)
        y = yref[0:MEMBERS, obs]
        innovation = obs_ref[j : j + 1, :] - yref[MEMBERS : MEMBERS + 1, obs]
        pull = jnp.sum(y * prec_ref[j : j + 1, :] * innovation, axis=1, keepdims=True)
        half = jnp.sum(root * pull, axis=0, keepdims=True)
        weight = jnp.sum(root * half, axis=1, keepdims=True)
        zz[j] = math.sqrt(MEMBERS - 1.0) * root
        shifts.append(weight)
    for block in range(5):
        lanes = pl.ds(block * 256, 256)
        own = (lane_index((MEMBERS, 256)) // 8) % 2 == 0
        cells = pert[0:MEMBERS, lanes]
        terms = []
        for j in range(2):
            base = pert[MEMBERS : MEMBERS + 1, lanes] + jnp.sum(cells * shifts[j], axis=0, keepdims=True)
            terms.append(base + mm(zz[j], cells))
        moved[:, lanes] = jnp.where(own, terms[0], terms[1])
    for tile in range(TILES):
        if tile < 9:
            value = moved[0:rows, tile * 128 : (tile + 1) * 128]
        elif tile == 9:
            rolled = pltpu.roll(moved[rows : 2 * rows, 0:128], 64, 1)
            value = jnp.where(low_half, moved[0:rows, 9 * 128 : 10 * 128], rolled)
        else:
            i = tile - 10
            first = moved[rows : 2 * rows, i * 128 : (i + 1) * 128]
            second = moved[rows : 2 * rows, (i + 1) * 128 : (i + 2) * 128]
            value = pltpu.roll(jnp.where(low_half, second, first), 64, 1)
        for s in range(4):
            out_ref[:, 0, pl.ds(s * PAIR + tile * 128, 128)] = value[s * 32 : (s + 1) * 32]


def restore_kernel(in_ref, out_ref):
    def body(s, carry):
        for y in range(4):
            tiles = [
                in_ref[pl.ds(y * 8, 8), 0, pl.ds(pl.multiple_of(s * PAIR + tile * 128, 128), 128)]
                for tile in range(TILES)
            ]
            moved = swap_blocks(jnp.stack(tiles, axis=0)).reshape(2 * LEVELS, GY)
            out_ref[2 * s, :, y * GY : (y + 1) * GY] = moved[0:LEVELS]
            out_ref[2 * s + 1, :, y * GY : (y + 1) * GY] = moved[LEVELS : 2 * LEVELS]
        return carry

    lax.fori_loop(0, 4, body, 0)


def params():
    return pltpu.CompilerParams(vmem_limit_bytes=VMEM_LIMIT)


def forecast(main, before, after, mixing, rate):
    return pl.pallas_call(
        forecast_kernel,
        out_shape=jax.ShapeDtypeStruct((128, 1, PAIR), F32),
        scratch_shapes=[
            pltpu.VMEM((2, 2, 24, PADDED, GY), F32),
            pltpu.VMEM((PADDED, 6 * PADDED), BF16),
            pltpu.VMEM((PADDED, GY), F32),
        ],
        compiler_params=params(),
        name="forecast",
    )(main, before, after, mixing, rate)


def analyse(cells, operator, observed, precisions):
    return pl.pallas_call(
        analysis_kernel,
        out_shape=jax.ShapeDtypeStruct((32, 1, 4 * PAIR), F32),
        scratch_shapes=[
            pltpu.VMEM((MEMBERS + 8, LANES), F32),
            pltpu.VMEM((2 * 128, LANES), F32),
            pltpu.VMEM((MEMBERS + 8, 2 * 128), F32),
            pltpu.VMEM((2, MEMBERS, MEMBERS), F32),
            pltpu.VMEM((2, MEMBERS, MEMBERS), F32),
            pltpu.VMEM((2, MEMBERS, MEMBERS), F32),
            pltpu.VMEM((MEMBERS, LANES), F32),
        ],
        compiler_params=params(),
        name="analysis",
    )(cells, operator, observed, precisions)


def restore(cells):
    return pl.pallas_call(
        restore_kernel,
        out_shape=jax.ShapeDtypeStruct((8, LEVELS, 4 * GY), F32),
        compiler_params=params(),
        name="restore",
    )(cells)


def prepare(blending_matrix, lateral_spreading):
    extra = PADDED - LEVELS
    mixing = jnp.tile(jnp.pad(blending_matrix, ((0, extra), (0, extra))), (1, 6))
    return mixing, jnp.pad(lateral_spreading, (0, extra))[:, None]


def shards(ensemble, blending_matrix, lateral_spreading, obs_op, obs_value, obs_precision):
    mixing, rate = prepare(blending_matrix, lateral_spreading)
    split = ensemble.reshape(4, 2, LEVELS, 4 * GY)
    main = lax.all_to_all(split, "x", split_axis=0, concat_axis=0, tiled=True)
    before = lax.ppermute(main[3], "zh", [(i, (i + 1) % 4) for i in range(4)])
    after = lax.ppermute(main[0], "zh", [((i + 1) % 4, i) for i in range(4)])
    sent = forecast(main, before, after, mixing, rate)
    owned = lax.all_to_all(sent, ("x", "y", "zl", "c"), split_axis=0, concat_axis=0, tiled=True)
    result = analyse(owned, obs_op, obs_value, obs_precision)
    returned = lax.all_to_all(result, ("y", "zl", "c"), split_axis=0, concat_axis=0, tiled=True)
    return restore(returned)


def solution(mesh):
    fine = Mesh(mesh.devices.reshape(4, 4, 2, 4, 4), ("y", "zl", "c", "zh", "x"))
    member, region = ("y", "zl", "c"), ("zh", "x")
    return jax.shard_map(
        shards,
        mesh=fine,
        in_specs=(
            P(member, None, region),
            P(),
            P(),
            P(region + member, None, None),
            P(region + member, None),
            P(region + member, None),
        ),
        out_specs=P(member, None, region),
        check_vma=False,
    )
```

time: 311 us -> 193 us (0.62)
  waiting for transfers between devices: 136 us -> 65.1 us
  matrix products: 45.1 us -> 0 us
  Pallas kernels: 0 us -> 42.3 us
  starting transfers between devices: 58.4 us -> 25.6 us
  local copies, waits for them, and re-layouts: 32.3 us -> 5.63 us
  blocking collectives: 36.1 us -> 53.4 us
    ppermute x8 -> x2, waiting for transfers between devices: 104 us -> 31.7 us  [the longest x1 26.2 us: shards(): after = lax.ppermute(main[0], 'zh', [((i + 1) % 4, i) for i in range(4)])]
    dot_general x88 -> x0, matrix products: 45.1 us -> none  [the longest x24 9.01 us: analyse(): jnp.dot(inv_iter, sqrt_iter, precision=HIGHEST, preferred_element_type=jn...]
    pallas_call x0 -> x3, Pallas kernels: none -> 42.3 us  [the longest x1 27 us: analyse(): pl.pallas_call(analysis_kernel, out_shape=jax.ShapeDtypeStruct((32, 1, 4...]
    ppermute x8 -> x2, starting transfers between devices: 40.2 us -> 18 us  [the longest x1 12.4 us: shards(): before = lax.ppermute(main[3], 'zh', [(i, (i + 1) % 4) for i in range(4)])]
    all_to_all x1 -> x2, blocking collectives: 36.1 us -> 53.4 us  [the longest x1 36.3 us: shards(): lax.all_to_all(result, ('y', 'zl', 'c'), split_axis=0, concat_axis=0, til...]
    reshape x6 -> x1, local copies, waits for them, and re-layouts: 12.4 us -> 0.96 us  [shards(): split = ensemble.reshape(4, 2, LEVELS, 4 * GY)]
    all_to_all x1, starting transfers between devices: 18.2 us -> 7.61 us  [shards(): lax.all_to_all(sent, ('x', 'y', 'zl', 'c'), split_axis=0, concat_axis=0,...]
    transpose x2 -> x0, local copies, waits for them, and re-layouts: 8.04 us -> none  [the longest x1 4.26 us: shards(): returned.reshape(members, patch_count, mem_dev, levels, patch_cols)]
  transfers between devices with their start and end apart: 9 -> 3, of which waited for: 7 -> 3; matrix products, arithmetic and copies ran while one was open for 1% -> 0% of each run, Pallas kernels for 0% -> 0%
where the time goes in v1:
time: 193 us; the launch traced here: 192 us
  waiting for transfers between devices  65.1 us (34%)
  blocking collectives  53.4 us (28%)
  Pallas kernels  42.3 us (22%)
  starting transfers between devices  25.6 us (13%)
  local copies, waits for them, and re-layouts  5.63 us (3%)
    all_to_all x1, blocking collectives, shards(): lax.all_to_all(result, ('y', 'zl', 'c'), split_axis=0, concat_axis=0, til...  36.3 us
    all_to_all x1, waiting for transfers between devices, shards(): lax.all_to_all(sent, ('x', 'y', 'zl', 'c'), split_axis=0, concat_axis=0,...  33.4 us
    pallas_call x1, Pallas kernels, analyse(): pl.pallas_call(analysis_kernel, out_shape=jax.ShapeDtypeStruct((32, 1, 4...  27 us
    ppermute x1, waiting for transfers between devices, shards(): after = lax.ppermute(main[0], 'zh', [((i + 1) % 4, i) for i in range(4)])  26.2 us
    all_to_all x1, blocking collectives, shards(): main = lax.all_to_all(split, 'x', split_axis=0, concat_axis=0, tiled=True)  17 us
    ppermute x1, starting transfers between devices, shards(): before = lax.ppermute(main[3], 'zh', [(i, (i + 1) % 4) for i in range(4)])  12.4 us
    pallas_call x1, Pallas kernels, forecast(): pl.pallas_call(forecast_kernel, out_shape=jax.ShapeDtypeStruct((128, 1, P...  12.1 us
    all_to_all x1, starting transfers between devices, shards(): lax.all_to_all(sent, ('x', 'y', 'zl', 'c'), split_axis=0, concat_axis=0,...  7.61 us
  transfers between devices with their start and end apart: 3, of which 3 were waited for; matrix products, arithmetic and copies ran while one was open for 0% of the time, Pallas kernels for 0%

profile of v1, /device:TPU:1, one launch (start us, length us, event | category | flops | bytes accessed | tf_op | source)
XLA Modules:
  0.0 192.2 jit_solution(7154968664029968977)
XLA Ops:
  0.0 2.0 %copy.25 = f32[8,76,512]{2,1,0:T(8,128)S(1)} copy(f32[8,76,512]{2,0,1:T(8,128)} %param.6) | data formatting | bytes 2490368 | tf_op args[0]
  2.0 1.0 copy.26
  3.0 17.0 %all_to_all.15 = f32[4,2,76,512]{3,1,2,0:T(2,128)S(1)} all-to-all(f32[4,2,76,512]{3,1,2,0:T(2,128)S(1)} %copy.26), channel_id=1, replica_groups=mesh['y'=4,'zl'=4,'c'=2,'zh'=4,'x'=4] {'x'}, dimensions={0} | all-to-all | bytes 2490368 | tf_op jit(solution)/shard_map/all_to_all | solution.py:299
  20.0 0.2 copy.30.main_ref
  20.3 0.0 copy-start.3
  20.3 0.0 copy-start.4
  20.4 12.4 %collective-permute-start = (f32[2,76,512]{2,1,0:T(8,128)S(1)}, f32[2,76,512]{2,1,0:T(8,128)S(1)}, u32[]{:S(2)}, u32[]{:S(2)}) collective-permute-start(f32[2,76,512]{2,1,0:T(8,128)S(1)} %get-tuple-element.6), channel_id=1, source_target_pairs={{0,4},{4,8},{8,12},{12,0},{1,5},{5,9},{9,13},{13,1},{2,6},{6,10},{... | collective-permute-start | bytes 933896 | tf_op jit(solution)/shard_map/ppermute | solution.py:300
  32.8 5.6 %collective-permute-start.1 = (f32[2,76,512]{2,1,0:T(8,128)S(1)}, f32[2,76,512]{2,1,0:T(8,128)S(1)}, u32[]{:S(2)}, u32[]{:S(2)}) collective-permute-start(f32[2,76,512]{2,1,0:T(8,128)S(1)} %get-tuple-element.5), channel_id=1, source_target_pairs={{4,0},{8,4},{12,8},{0,12},{5,1},{9,5},{13,9},{1,13},{6,2},{10,6},{... | collective-permute-start | bytes 933896 | tf_op jit(solution)/shard_map/ppermute | solution.py:301
  38.4 0.1 copy.35
  38.5 0.1 copy.31.mix_ref
  38.6 0.0 copy-done.4
  38.6 0.1 copy.32.rate_ref
  38.7 5.5 %collective-permute-done.prev_ref = f32[2,76,512]{2,1,0:T(8,128)S(1)} collective-permute-done((f32[2,76,512]{2,1,0:T(8,128)S(1)}, f32[2,76,512]{2,1,0:T(8,128)S(1)}, u32[]{:S(2)}, u32[]{:S(2)}) %collective-permute-start) | collective-permute-done | bytes 311328 | tf_op jit(solution)/shard_map/ppermute | solution.py:300
  44.2 26.2 %collective-permute-done.1.next_ref = f32[2,76,512]{2,1,0:T(8,128)S(1)} collective-permute-done((f32[2,76,512]{2,1,0:T(8,128)S(1)}, f32[2,76,512]{2,1,0:T(8,128)S(1)}, u32[]{:S(2)}, u32[]{:S(2)}) %collective-permute-start.1) | collective-permute-done | bytes 311328 | tf_op jit(solution)/shard_map/ppermute | solution.py:301
  70.4 12.1 %forecast.1 = f32[128,1,2432]{2,1,0:T(1,128)} custom-call(f32[4,2,76,512]{3,2,1,0:T(8,128)S(1)} %copy.30.main_ref, f32[2,76,512]{2,1,0:T(8,128)S(1)} %collective-permute-done.prev_ref, f32[2,76,512]{2,1,0:T(8,128)S(1)} %collective-permute-done.1.next_ref, f32[80,480]{1,0:T(8,128)S(1)} %copy.31.mix_ref, f32[80,1]{1,0:T(8,128)S(1)} %copy.32.rate_ref), custom_call_target="tpu_custom_call" | custom-call | tf_op jit(solution)/shard_map/forecast/pallas_call | solution.py:250
  82.5 7.6 %all-to-all-start.1 = ((f32[128,1,2432]{2,1,0:T(1,128)}), f32[128,1,2432]{2,1,0:T(1,128)S(1)}, u32[]{:S(2)}, u32[]{:S(2)}) async-start(f32[128,1,2432]{2,1,0:T(1,128)} %forecast.1), calls=%async_computation.1 | async-start | bytes 2490368 | tf_op jit(solution)/shard_map/all_to_all | solution.py:303
  90.1 0.0 copy-start
  90.2 0.0 copy-start.1
  90.2 0.2 copy.33.op_ref
  90.4 33.4 %all-to-all-done.1.x_ref = f32[128,1,2432]{2,1,0:T(1,128)S(1)} async-done(((f32[128,1,2432]{2,1,0:T(1,128)}), f32[128,1,2432]{2,1,0:T(1,128)S(1)}, u32[]{:S(2)}, u32[]{:S(2)}) %all-to-all-start.1) | async-done | bytes 1245216 | tf_op jit(solution)/shard_map/all_to_all | solution.py:303
  123.9 27.0 %analysis.1 = f32[32,1,9728]{2,1,0:T(1,128)S(1)} custom-call(f32[128,1,2432]{2,1,0:T(1,128)S(1)} %all-to-all-done.1.x_ref, f32[2,128,608]{2,1,0:T(8,128)S(1)} %copy.33.op_ref, f32[2,128]{1,0:T(2,128)S(1)} %copy-done, f32[2,128]{1,0:T(2,128)S(1)} %copy-done.1), custom_call_target="tpu_custom_call" | custom-call | tf_op jit(solution)/shard_map/analysis/pallas_call | solution.py:264
  150.8 36.3 %all_to_all.16.in_ref = f32[32,1,9728]{2,1,0:T(1,128)S(1)} all-to-all(f32[32,1,9728]{2,1,0:T(1,128)S(1)} %analysis.1), channel_id=1, replica_groups=mesh['y'=4,'zl'=4,'c'=2,'zh'=4,'x'=4] {'y','zl','c'}, dimensions={0} | all-to-all | bytes 2490368 | tf_op jit(solution)/shard_map/all_to_all | solution.py:305
  187.2 3.2 %restore.1 = f32[8,76,512]{2,1,0:T(8,128)S(1)} custom-call(f32[32,1,9728]{2,1,0:T(1,128)S(1)} %all_to_all.16.in_ref), custom_call_target="tpu_custom_call" | custom-call | tf_op jit(solution)/shard_map/restore/pallas_call | solution.py:282
  190.4 1.8 copy.34
  (9 shorter events, 0.1 us)
Async XLA Ops:
  20.3 18.1 %copy-start.3 = (f32[76,76]{1,0:T(8,128)S(1)}, f32[76,76]{1,0:T(8,128)}, u32[]{:S(2)}) copy-start(f32[76,76]{1,0:T(8,128)} %param.7) | copy-start | bytes 69316
  20.3 18.3 %copy-start.4 = (f32[76]{0:T(128)S(1)}, f32[76]{0:T(128)}, u32[]{:S(2)}) copy-start(f32[76]{0:T(128)} %param.8) | copy-start | bytes 916
  20.4 23.8 %collective-permute-start = (f32[2,76,512]{2,1,0:T(8,128)S(1)}, f32[2,76,512]{2,1,0:T(8,128)S(1)}, u32[]{:S(2)}, u32[]{:S(2)}) collective-permute-start(f32[2,76,512]{2,1,0:T(8,128)S(1)} %get-tuple-element.6), channel_id=1, source_target_pairs={{0,4},{4,8},{8,12},{12,0},{1,5},{5,9},{9,13},{13,1},{2,6},{6,10},{... | collective-permute-start | bytes 933896 | tf_op jit(solution)/shard_map/ppermute | solution.py:300
  32.8 37.6 %collective-permute-start.1 = (f32[2,76,512]{2,1,0:T(8,128)S(1)}, f32[2,76,512]{2,1,0:T(8,128)S(1)}, u32[]{:S(2)}, u32[]{:S(2)}) collective-permute-start(f32[2,76,512]{2,1,0:T(8,128)S(1)} %get-tuple-element.5), channel_id=1, source_target_pairs={{4,0},{8,4},{12,8},{0,12},{5,1},{9,5},{13,9},{1,13},{6,2},{10,6},{... | collective-permute-start | bytes 933896 | tf_op jit(solution)/shard_map/ppermute | solution.py:301
  82.5 7.6 %copy-start.2 = (f32[2,128,608]{1,2,0:T(8,128)S(1)}, f32[2,128,608]{1,2,0:T(8,128)}, u32[]{:S(2)}) copy-start(f32[2,128,608]{1,2,0:T(8,128)} %param.9) | copy-start | bytes 1867780
  82.5 41.3 %all-to-all-start.1 = ((f32[128,1,2432]{2,1,0:T(1,128)}), f32[128,1,2432]{2,1,0:T(1,128)S(1)}, u32[]{:S(2)}, u32[]{:S(2)}) async-start(f32[128,1,2432]{2,1,0:T(1,128)} %forecast.1), calls=%async_computation.1 | async-start | bytes 2490368 | tf_op jit(solution)/shard_map/all_to_all | solution.py:303
  90.1 33.7 %copy-start = (f32[2,128]{1,0:T(2,128)S(1)}, f32[2,128]{1,0:T(2,128)}, u32[]{:S(2)}) copy-start(f32[2,128]{1,0:T(2,128)} %obs_ref.1) | copy-start | bytes 3076
  90.2 33.7 %copy-start.1 = (f32[2,128]{1,0:T(2,128)S(1)}, f32[2,128]{1,0:T(2,128)}, u32[]{:S(2)}) copy-start(f32[2,128]{1,0:T(2,128)} %prec_ref.1) | copy-start | bytes 3076

commit v2 on v1

v2 whole, which is shorter than its diff:
```python
import math

import jax
import jax.numpy as jnp
from jax import lax
from jax.experimental import pallas as pl
from jax.experimental.pallas import tpu as pltpu
from jax.sharding import Mesh, PartitionSpec as P

F32 = jnp.float32
BF16 = jnp.bfloat16
HIGHEST = lax.Precision.HIGHEST
LEVELS = 76
PADDED = 80
GY = 128
NSTEP = 4
ITERS = 12
MEMBERS = 256
BLOCKS = 5
WIDTH = BLOCKS * 128
CHUNK = 2 * WIDTH
VMEM_LIMIT = 32 * 1024 * 1024


def lane_index(shape):
    return lax.broadcasted_iota(jnp.int32, shape, len(shape) - 1)


def split3(x):
    high = x.astype(BF16)
    rest = x - high.astype(F32)
    mid = rest.astype(BF16)
    low = (rest - mid.astype(F32)).astype(BF16)
    return high, mid, low


def swap_blocks(x):
    sub = lax.broadcasted_iota(jnp.int32, x.shape, 1)
    block = lane_index(x.shape) // 16
    for bit in (1, 2, 4):
        up = (sub & bit) != 0
        keep = up == ((block & bit) != 0)
        lanes = 16 * bit
        lower = pltpu.roll(pltpu.roll(x, 8 - bit, 1), lanes, 2)
        if bit == 4:
            other = lower
        else:
            upper = pltpu.roll(pltpu.roll(x, bit, 1), 128 - lanes, 2)
            other = jnp.where(up, upper, lower)
        x = jnp.where(keep, x, other)
    return x


def forecast_kernel(main_ref, prev_ref, next_ref, mix_ref, rate_ref, out0_ref, out1_ref, state, mix, rate):
    wide = mix_ref[...]
    high, mid, low = split3(wide)
    part = lane_index(wide.shape) // PADDED
    pick_mid = (part == 2) | (part == 3)
    mix[...] = jnp.where(
        pick_mid, mid.astype(F32), jnp.where(part == 5, low.astype(F32), high.astype(F32))
    ).astype(BF16)
    rate[...] = jnp.broadcast_to(rate_ref[...], (PADDED, GY))
    pad = jnp.zeros((PADDED - LEVELS, GY), F32)
    for m in range(2):
        for row in range(24):
            cols = pl.ds((row % 4) * GY, GY)
            if row < 4:
                cells = prev_ref[m, :, cols]
            elif row < 20:
                cells = main_ref[row // 4 - 1, m, :, cols]
            else:
                cells = next_ref[m, :, cols]
            state[0, m, row, 0:LEVELS, :] = cells
            state[0, m, row, LEVELS:PADDED, :] = pad

    def advance(now, m, row):
        centre = [state[now, m, row + i] for i in range(2)]
        before = state[now, m, row - 1]
        after = state[now, m, row + 2]
        parts = split3(jnp.concatenate(centre, axis=1))
        stacked = jnp.concatenate([parts[i] for i in (0, 1, 0, 1, 2, 0)], axis=0)
        coupled = jnp.dot(mix[...], stacked, preferred_element_type=F32)
        result = []
        for i in range(2):
            cells = centre[i]
            around = (centre[1] + before) if i == 0 else (after + centre[0])
            laplace = (
                around + pltpu.roll(cells, GY - 1, 1) + pltpu.roll(cells, 1, 1) - 4.0 * cells
            )
            pushed = jnp.tanh(coupled[:, i * GY : (i + 1) * GY])
            result.append(cells + rate[...] * laplace + 0.3 * pushed)
        return result

    for step in range(NSTEP - 1):
        now = step % 2

        def body(pair, carry, now=now, step=step):
            row = step + 1 + 2 * pair
            for m in range(2):
                result = advance(now, m, row)
                state[1 - now, m, row] = result[0]
                state[1 - now, m, row + 1] = result[1]
            return carry

        lax.fori_loop(0, (22 - 2 * step) // 2, body, 0)

    second = (lane_index((8, GY)) // 8) % 2 == 1

    def last(pair, carry):
        row = 4 + 2 * pair
        for m in range(2):
            result = advance((NSTEP - 1) % 2, m, row)
            for i in range(2):
                start = (2 * pair + i) * 8
                low = result[i].reshape(BLOCKS, 2, 8, GY)
                for j, out_ref in enumerate((out0_ref, out1_ref)):
                    tiles = []
                    for k in range(BLOCKS):
                        if j == 0:
                            tiles.append(jnp.where(second, pltpu.roll(low[k, 1], 8, 1), low[k, 0]))
                        else:
                            tiles.append(jnp.where(second, low[k, 1], pltpu.roll(low[k, 0], GY - 8, 1)))
                    moved = swap_blocks(jnp.stack(tiles, axis=0))
                    for k in range(BLOCKS):
                        out_ref[pl.ds(start, 8), 0, pl.ds(m * WIDTH + k * 128, 128)] = moved[k]
        return carry

    lax.fori_loop(0, 8, last, 0)


def analysis_kernel(x_ref, op_ref, obs_ref, prec_ref, out_ref, pert, wide, yref, rr, zz, ff):
    rows = 128
    take = lax.broadcasted_iota(jnp.int32, (128, 128), 0)
    put = lane_index((128, 128))
    source = ((put // 8) % 2) * 64 + (put // 16) * 8 + put % 8
    order = jnp.where(take == source, 1.0, 0.0).astype(BF16)
    for k in range(BLOCKS):
        lanes = pl.ds(k * 128, 128)
        halves = [x_ref[:, 0, pl.ds(m * WIDTH + k * 128, 128)] for m in range(2)]
        mean = (
            jnp.sum(halves[0], axis=0, keepdims=True) + jnp.sum(halves[1], axis=0, keepdims=True)
        ) / MEMBERS
        for m in range(2):
            pert[m * rows : (m + 1) * rows, lanes] = halves[m] - mean
        pert[MEMBERS : MEMBERS + 8, lanes] = jnp.broadcast_to(mean, (8, 128))
        width = 128 if k < BLOCKS - 1 else 8 * LEVELS - 512
        grown = [
            jnp.dot(p, order[0:width], preferred_element_type=F32)
            for p in split3(op_ref[0, :, pl.ds(k * 128, width)])
        ]
        wide[:, lanes] = (grown[0] + grown[1]) + grown[2]

    yref[...] = lax.dot_general(
        pert[...], wide[...], (((1,), (1,)), ((), ())), precision=HIGHEST, preferred_element_type=F32
    )
    eye = jnp.where(
        lax.broadcasted_iota(jnp.int32, (MEMBERS, MEMBERS), 0) == lane_index((MEMBERS, MEMBERS)), 1.0, 0.0
    )

    def mm(a, b):
        return jnp.dot(a, b, precision=HIGHEST, preferred_element_type=F32)

    y = yref[0:MEMBERS]
    weighted = y * prec_ref[0]
    gram = lax.dot_general(
        weighted, y, (((1,), (1,)), ((), ())), precision=HIGHEST, preferred_element_type=F32
    )
    system = (MEMBERS - 1.0) * eye + gram
    norm = jnp.sqrt(jnp.sum(jnp.sum(system * system, axis=0, keepdims=True), axis=1, keepdims=True))
    start = system / norm
    factor = 0.5 * (3.0 * eye - start)
    zz[...] = factor
    rr[...] = mm(start, factor)

    def body(step, carry):
        ff[...] = 0.5 * (3.0 * eye - mm(zz[...], rr[...]))
        rr[...] = mm(rr[...], ff[...])
        zz[...] = mm(ff[...], zz[...])
        return carry

    lax.fori_loop(0, ITERS - 2, body, 0)
    factor = 0.5 * (3.0 * eye - mm(zz[...], rr[...]))
    root = mm(factor, zz[...]) / jnp.sqrt(norm)
    innovation = obs_ref[0] - yref[MEMBERS : MEMBERS + 1]
    pull = jnp.sum(y * prec_ref[0] * innovation, axis=1, keepdims=True)
    half = jnp.sum(root * pull, axis=0, keepdims=True)
    shift = jnp.sum(root * half, axis=1, keepdims=True)
    zz[...] = math.sqrt(MEMBERS - 1.0) * root
    for start, size in ((0, 256), (256, 256), (512, 128)):
        lanes = pl.ds(start, size)
        cells = pert[0:MEMBERS, lanes]
        base = pert[MEMBERS : MEMBERS + 1, lanes] + jnp.sum(cells * shift, axis=0, keepdims=True)
        moved = base + mm(zz[...], cells)
        for m in range(2):
            for s in range(4):
                first = m * rows + s * 32
                out_ref[:, 0, pl.ds(s * CHUNK + m * WIDTH + start, size)] = moved[first : first + 32]


def restore_kernel(in0_ref, in1_ref, out_ref):
    second = (lane_index((BLOCKS, 8, GY)) // 8) % 2 == 1

    def body(s, carry):
        for m in range(2):
            for y in range(4):
                groups = []
                for in_ref in (in0_ref, in1_ref):
                    tiles = [
                        in_ref[
                            pl.ds(y * 8, 8),
                            0,
                            pl.ds(pl.multiple_of(s * CHUNK + m * WIDTH + k * 128, 128), 128),
                        ]
                        for k in range(BLOCKS)
                    ]
                    groups.append(swap_blocks(jnp.stack(tiles, axis=0)))
                even = jnp.where(second, pltpu.roll(groups[1], 8, 2), groups[0])
                odd = jnp.where(second, groups[1], pltpu.roll(groups[0], GY - 8, 2))
                cols = pl.ds(y * GY, GY)
                for k in range(BLOCKS):
                    out_ref[2 * s + m, pl.ds(16 * k, 8), cols] = even[k]
                    last = 8 if k < BLOCKS - 1 else LEVELS - 72
                    out_ref[2 * s + m, pl.ds(16 * k + 8, last), cols] = odd[k, 0:last]
        return carry

    lax.fori_loop(0, 4, body, 0)


def params():
    return pltpu.CompilerParams(vmem_limit_bytes=VMEM_LIMIT)


def forecast(main, before, after, mixing, rate):
    return pl.pallas_call(
        forecast_kernel,
        out_shape=[jax.ShapeDtypeStruct((128, 1, CHUNK), F32)] * 2,
        scratch_shapes=[
            pltpu.VMEM((2, 2, 24, PADDED, GY), F32),
            pltpu.VMEM((PADDED, 6 * PADDED), BF16),
            pltpu.VMEM((PADDED, GY), F32),
        ],
        compiler_params=params(),
        name="forecast",
    )(main, before, after, mixing, rate)


def analyse(cells, operator, observed, precisions):
    return pl.pallas_call(
        analysis_kernel,
        out_shape=jax.ShapeDtypeStruct((32, 1, 4 * CHUNK), F32),
        scratch_shapes=[
            pltpu.VMEM((MEMBERS + 8, WIDTH), F32),
            pltpu.VMEM((128, WIDTH), F32),
            pltpu.VMEM((MEMBERS + 8, 128), F32),
            pltpu.VMEM((MEMBERS, MEMBERS), F32),
            pltpu.VMEM((MEMBERS, MEMBERS), F32),
            pltpu.VMEM((MEMBERS, MEMBERS), F32),
        ],
        compiler_params=params(),
        cost_estimate=pl.CostEstimate(
            flops=36 * 6 * 2 * MEMBERS**3, bytes_accessed=4 * 2**20, transcendentals=0
        ),
        name="analysis",
    )(cells, operator, observed, precisions)


def restore(first, second):
    return pl.pallas_call(
        restore_kernel,
        out_shape=jax.ShapeDtypeStruct((8, LEVELS, 4 * GY), F32),
        compiler_params=params(),
        name="restore",
    )(first, second)


def prepare(blending_matrix, lateral_spreading):
    extra = PADDED - LEVELS
    mixing = jnp.tile(jnp.pad(blending_matrix, ((0, extra), (0, extra))), (1, 6))
    return mixing, jnp.pad(lateral_spreading, (0, extra))[:, None]


def shards(ensemble, blending_matrix, lateral_spreading, obs_op, obs_value, obs_precision):
    mixing, rate = prepare(blending_matrix, lateral_spreading)
    split = ensemble.reshape(4, 2, LEVELS, 4 * GY)
    main = lax.all_to_all(split, "x", split_axis=0, concat_axis=0, tiled=True)
    before = lax.ppermute(main[3], "zh", [(i, (i + 1) % 4) for i in range(4)])
    after = lax.ppermute(main[0], "zh", [((i + 1) % 4, i) for i in range(4)])
    sent = forecast(main, before, after, mixing, rate)
    owned = [
        lax.all_to_all(part, ("x", "y", "zl", "c"), split_axis=0, concat_axis=0, tiled=True)
        for part in sent
    ]
    returned = []
    for j in range(2):
        result = analyse(
            owned[j], obs_op[j : j + 1], obs_value[j : j + 1, None], obs_precision[j : j + 1, None]
        )
        returned.append(
            lax.all_to_all(result, ("y", "zl", "c"), split_axis=0, concat_axis=0, tiled=True)
        )
    return restore(*returned)


def solution(mesh):
    fine = Mesh(mesh.devices.reshape(4, 4, 2, 4, 4), ("y", "zl", "c", "zh", "x"))
    member, region = ("y", "zl", "c"), ("zh", "x")
    return jax.shard_map(
        shards,
        mesh=fine,
        in_specs=(
            P(member, None, region),
            P(),
            P(),
            P(region + member, None, None),
            P(region + member, None),
            P(region + member, None),
        ),
        out_specs=P(member, None, region),
        check_vma=False,
    )
```

time: 193 us -> 196 us (1.016)
  waiting for transfers between devices: 65.1 us -> 43.1 us
  blocking collectives: 53.4 us -> 68.6 us
  Pallas kernels: 42.3 us -> 48.5 us
  starting transfers between devices: 25.6 us -> 29.6 us
    all_to_all x0 -> x1, blocking collectives: none -> 28.5 us  [shards(): lax.all_to_all(part, ('x', 'y', 'zl', 'c'), split_axis=0, concat_axis=0,...]
    all_to_all x1 -> x2, waiting for transfers between devices: 33.4 us -> 11.5 us  [the longest x1 6 us: shards(): lax.all_to_all(part, ('x', 'y', 'zl', 'c'), split_axis=0, concat_axis=0,...]
    all_to_all x1, blocking collectives: 36.3 us -> 23.1 us  [shards(): lax.all_to_all(result, ('y', 'zl', 'c'), split_axis=0, concat_axis=0, til...]
    all_to_all x1 -> x2, starting transfers between devices: 7.61 us -> 11.6 us  [the longest x1 6.92 us: shards(): lax.all_to_all(part, ('x', 'y', 'zl', 'c'), split_axis=0, concat_axis=0,...]
    pallas_call x1, Pallas kernels: 3.24 us -> 7.14 us  [restore(): pl.pallas_call(restore_kernel, out_shape=jax.ShapeDtypeStruct((8, LEVELS,...]
    pallas_call x1 -> x2, Pallas kernels: 27 us -> 28.8 us  [analyse(): pl.pallas_call(analysis_kernel, out_shape=jax.ShapeDtypeStruct((32, 1, 4...]
  transfers between devices with their start and end apart: 3 -> 4, of which waited for: 3 -> 4; matrix products, arithmetic and copies ran while one was open for 0% -> 0% of each run, Pallas kernels for 0% -> 15%
where the time goes in v2:
time: 196 us
  blocking collectives  68.6 us (35%)
  Pallas kernels  48.5 us (25%)
  waiting for transfers between devices  43.1 us (22%)
  starting transfers between devices  29.6 us (15%)
  local copies, waits for them, and re-layouts  5.76 us (3%)
    pallas_call x2, Pallas kernels, analyse(): pl.pallas_call(analysis_kernel, out_shape=jax.ShapeDtypeStruct((32, 1, 4...  28.8 us
    all_to_all x1, blocking collectives, shards(): lax.all_to_all(part, ('x', 'y', 'zl', 'c'), split_axis=0, concat_axis=0,...  28.5 us
    ppermute x1, waiting for transfers between devices, shards(): after = lax.ppermute(main[0], 'zh', [((i + 1) % 4, i) for i in range(4)])  26.2 us
    all_to_all x1, blocking collectives, shards(): lax.all_to_all(result, ('y', 'zl', 'c'), split_axis=0, concat_axis=0, til...  23.1 us
    all_to_all x1, blocking collectives, shards(): main = lax.all_to_all(split, 'x', split_axis=0, concat_axis=0, tiled=True)  17 us
    pallas_call x1, Pallas kernels, forecast(): pl.pallas_call(forecast_kernel, out_shape=[jax.ShapeDtypeStruct((128, 1,...  12.6 us
    ppermute x1, starting transfers between devices, shards(): before = lax.ppermute(main[3], 'zh', [(i, (i + 1) % 4) for i in range(4)])  12.4 us
    pallas_call x1, Pallas kernels, restore(): pl.pallas_call(restore_kernel, out_shape=jax.ShapeDtypeStruct((8, LEVELS,...  7.14 us
  transfers between devices with their start and end apart: 4, of which 4 were waited for; matrix products, arithmetic and copies ran while one was open for 0% of the time, Pallas kernels for 15%

profile of v2, /device:TPU:1, one launch (start us, length us, event | category | flops | bytes accessed | tf_op | source)
XLA Modules:
  0.0 195.8 jit_solution(18080225284254633293)
XLA Ops:
  0.0 2.0 %copy.28 = f32[8,76,512]{2,1,0:T(8,128)S(1)} copy(f32[8,76,512]{2,0,1:T(8,128)} %param.6) | data formatting | bytes 2490368 | tf_op args[0]
  2.0 1.0 copy.29
  3.0 17.0 %all_to_all.25 = f32[4,2,76,512]{3,1,2,0:T(2,128)S(1)} all-to-all(f32[4,2,76,512]{3,1,2,0:T(2,128)S(1)} %copy.29), channel_id=1, replica_groups=mesh['y'=4,'zl'=4,'c'=2,'zh'=4,'x'=4] {'x'}, dimensions={0} | all-to-all | bytes 2490368 | tf_op jit(solution)/shard_map/all_to_all | solution.py:285
  20.0 0.2 copy.33.main_ref
  20.3 12.4 %collective-permute-start = (f32[2,76,512]{2,1,0:T(8,128)S(1)}, f32[2,76,512]{2,1,0:T(8,128)S(1)}, u32[]{:S(2)}, u32[]{:S(2)}) collective-permute-start(f32[2,76,512]{2,1,0:T(8,128)S(1)} %get-tuple-element.10), channel_id=1, source_target_pairs={{0,4},{4,8},{8,12},{12,0},{1,5},{5,9},{9,13},{13,1},{2,6},{6,10},{... | collective-permute-start | bytes 933896 | tf_op jit(solution)/shard_map/ppermute | solution.py:286
  32.8 5.6 %collective-permute-start.1 = (f32[2,76,512]{2,1,0:T(8,128)S(1)}, f32[2,76,512]{2,1,0:T(8,128)S(1)}, u32[]{:S(2)}, u32[]{:S(2)}) collective-permute-start(f32[2,76,512]{2,1,0:T(8,128)S(1)} %get-tuple-element.9), channel_id=1, source_target_pairs={{4,0},{8,4},{12,8},{0,12},{5,1},{9,5},{13,9},{1,13},{6,2},{10,6},{... | collective-permute-start | bytes 933896 | tf_op jit(solution)/shard_map/ppermute | solution.py:287
  38.3 0.1 copy.41
  38.5 0.1 copy.34.mix_ref
  38.6 0.1 copy.35.rate_ref
  38.7 5.5 %collective-permute-done.prev_ref = f32[2,76,512]{2,1,0:T(8,128)S(1)} collective-permute-done((f32[2,76,512]{2,1,0:T(8,128)S(1)}, f32[2,76,512]{2,1,0:T(8,128)S(1)}, u32[]{:S(2)}, u32[]{:S(2)}) %collective-permute-start) | collective-permute-done | bytes 311328 | tf_op jit(solution)/shard_map/ppermute | solution.py:286
  44.2 26.2 %collective-permute-done.1.next_ref = f32[2,76,512]{2,1,0:T(8,128)S(1)} collective-permute-done((f32[2,76,512]{2,1,0:T(8,128)S(1)}, f32[2,76,512]{2,1,0:T(8,128)S(1)}, u32[]{:S(2)}, u32[]{:S(2)}) %collective-permute-start.1) | collective-permute-done | bytes 311328 | tf_op jit(solution)/shard_map/ppermute | solution.py:287
  70.4 12.6 %forecast.1 = (f32[128,1,1280]{2,1,0:T(1,128)}, f32[128,1,1280]{2,1,0:T(1,128)S(1)}) custom-call(f32[4,2,76,512]{3,2,1,0:T(8,128)S(1)} %copy.33.main_ref, f32[2,76,512]{2,1,0:T(8,128)S(1)} %collective-permute-done.prev_ref, f32[2,76,512]{2,1,0:T(8,128)S(1)} %collective-permute-done.1.next_ref, f32[80,480]{1,0:T(8,128)S(1)} %copy.34.mix_ref, ...), custom_call_target="tpu_custom_call" | custom-call | tf_op jit(solution)/shard_map/forecast/pallas_call | solution.py:234
  82.9 28.5 %all_to_all.26.x_ref = f32[128,1,1280]{2,1,0:T(1,128)S(1)} all-to-all(f32[128,1,1280]{2,1,0:T(1,128)S(1)} %get-tuple-element.8), channel_id=1, replica_groups=mesh['y'=4,'zl'=4,'c'=2,'zh'=4,'x'=4] {'x','y','zl','c'}, dimensions={0} | all-to-all | bytes 1310720 | tf_op jit(solution)/shard_map/all_to_all | solution.py:290
  111.4 6.9 %all-to-all-start.1 = ((f32[128,1,1280]{2,1,0:T(1,128)}), f32[128,1,1280]{2,1,0:T(1,128)S(1)}, u32[]{:S(2)}, u32[]{:S(2)}) async-start(f32[128,1,1280]{2,1,0:T(1,128)} %get-tuple-element.7), calls=%async_computation.1 | async-start | bytes 1310720 | tf_op jit(solution)/shard_map/all_to_all | solution.py:290
  118.4 0.2 copy.40.op_ref
  118.6 14.8 %analysis.3 = f32[32,1,5120]{2,1,0:T(1,128)} custom-call(f32[128,1,1280]{2,1,0:T(1,128)S(1)} %all_to_all.26.x_ref, f32[1,128,608]{2,1,0:T(8,128)S(1)} %copy.40.op_ref, f32[1,1,128]{2,1,0:T(1,128)S(1)} %get-tuple-element.18.obs_ref, f32[1,1,128]{2,1,0:T(1,128)S(1)} %get-tuple-element.13.prec_ref), custom_call_target="tpu_custom_call" | custom-call | flops 7247757312 | bytes 4194304 | tf_op jit(solution)/shard_map/analysis/pallas_call | solution.py:248
  133.4 6.0 %all-to-all-done.1.x_ref = f32[128,1,1280]{2,1,0:T(1,128)S(1)} async-done(((f32[128,1,1280]{2,1,0:T(1,128)}), f32[128,1,1280]{2,1,0:T(1,128)S(1)}, u32[]{:S(2)}, u32[]{:S(2)}) %all-to-all-start.1) | async-done | bytes 655392 | tf_op jit(solution)/shard_map/all_to_all | solution.py:290
  139.4 4.7 %all-to-all-start.4 = ((f32[32,1,5120]{2,1,0:T(1,128)}), f32[32,1,5120]{2,1,0:T(1,128)S(1)}, u32[]{:S(2)}, u32[]{:S(2)}) async-start(f32[32,1,5120]{2,1,0:T(1,128)} %analysis.3), calls=%async_computation.4 | async-start | bytes 1310720 | tf_op jit(solution)/shard_map/all_to_all | solution.py:299
  144.1 0.2 copy.39.op_ref
  144.3 14.0 %analysis.2 = f32[32,1,5120]{2,1,0:T(1,128)S(1)} custom-call(f32[128,1,1280]{2,1,0:T(1,128)S(1)} %all-to-all-done.1.x_ref, f32[1,128,608]{2,1,0:T(8,128)S(1)} %copy.39.op_ref, f32[1,1,128]{2,1,0:T(1,128)S(1)} %get-tuple-element.17.obs_ref, f32[1,1,128]{2,1,0:T(1,128)S(1)} %get-tuple-element.14.prec_ref), custom_call_target="tpu_custom_call" | custom-call | flops 7247757312 | bytes 4194304 | tf_op jit(solution)/shard_map/analysis/pallas_call | solution.py:248
  158.3 5.5 %all-to-all-done.4.in1_ref = f32[32,1,5120]{2,1,0:T(1,128)S(1)} async-done(((f32[32,1,5120]{2,1,0:T(1,128)}), f32[32,1,5120]{2,1,0:T(1,128)S(1)}, u32[]{:S(2)}, u32[]{:S(2)}) %all-to-all-start.4) | async-done | bytes 655392 | tf_op jit(solution)/shard_map/all_to_all | solution.py:299
  163.8 23.1 %all_to_all.27.in0_ref = f32[32,1,5120]{2,1,0:T(1,128)S(1)} all-to-all(f32[32,1,5120]{2,1,0:T(1,128)S(1)} %analysis.2), channel_id=1, replica_groups=mesh['y'=4,'zl'=4,'c'=2,'zh'=4,'x'=4] {'y','zl','c'}, dimensions={0} | all-to-all | bytes 1310720 | tf_op jit(solution)/shard_map/all_to_all | solution.py:299
  186.9 7.1 %restore.1 = f32[8,76,512]{2,1,0:T(8,128)S(1)} custom-call(f32[32,1,5120]{2,1,0:T(1,128)S(1)} %all_to_all.27.in0_ref, f32[32,1,5120]{2,1,0:T(1,128)S(1)} %all-to-all-done.4.in1_ref), custom_call_target="tpu_custom_call" | custom-call | tf_op jit(solution)/shard_map/restore/pallas_call | solution.py:268
  194.1 1.8 copy.38
  (16 shorter events, 0.1 us)
Async XLA Ops:
  20.0 18.3 %copy-start.1 = (f32[76,76]{1,0:T(8,128)S(1)}, f32[76,76]{1,0:T(8,128)}, u32[]{:S(2)}) copy-start(f32[76,76]{1,0:T(8,128)} %param.7) | copy-start | bytes 69316
  20.3 18.3 %copy-start.4 = (f32[76]{0:T(128)S(1)}, f32[76]{0:T(128)}, u32[]{:S(2)}) copy-start(f32[76]{0:T(128)} %param.8) | copy-start | bytes 916
  20.3 23.8 %collective-permute-start = (f32[2,76,512]{2,1,0:T(8,128)S(1)}, f32[2,76,512]{2,1,0:T(8,128)S(1)}, u32[]{:S(2)}, u32[]{:S(2)}) collective-permute-start(f32[2,76,512]{2,1,0:T(8,128)S(1)} %get-tuple-element.10), channel_id=1, source_target_pairs={{0,4},{4,8},{8,12},{12,0},{1,5},{5,9},{9,13},{13,1},{2,6},{6,10},{... | collective-permute-start | bytes 933896 | tf_op jit(solution)/shard_map/ppermute | solution.py:286
  32.8 37.6 %collective-permute-start.1 = (f32[2,76,512]{2,1,0:T(8,128)S(1)}, f32[2,76,512]{2,1,0:T(8,128)S(1)}, u32[]{:S(2)}, u32[]{:S(2)}) collective-permute-start(f32[2,76,512]{2,1,0:T(8,128)S(1)} %get-tuple-element.9), channel_id=1, source_target_pairs={{4,0},{8,4},{12,8},{0,12},{5,1},{9,5},{13,9},{1,13},{6,2},{10,6},{... | collective-permute-start | bytes 933896 | tf_op jit(solution)/shard_map/ppermute | solution.py:287
  82.9 35.4 %copy-start = (f32[2,128,608]{1,2,0:T(8,128)S(1)}, f32[2,128,608]{1,2,0:T(8,128)}, u32[]{:S(2)}) copy-start(f32[2,128,608]{1,2,0:T(8,128)} %param.9) | copy-start | bytes 1867780
  111.4 7.2 %copy-start.2 = (f32[2,128]{1,0:T(2,128)S(1)}, f32[2,128]{1,0:T(2,128)}, u32[]{:S(2)}) copy-start(f32[2,128]{1,0:T(2,128)} %param.11) | copy-start | bytes 3076
  111.4 7.2 %copy-start.3 = (f32[2,128]{1,0:T(2,128)S(1)}, f32[2,128]{1,0:T(2,128)}, u32[]{:S(2)}) copy-start(f32[2,128]{1,0:T(2,128)} %param.10) | copy-start | bytes 3076
  111.4 28.0 %all-to-all-start.1 = ((f32[128,1,1280]{2,1,0:T(1,128)}), f32[128,1,1280]{2,1,0:T(1,128)S(1)}, u32[]{:S(2)}, u32[]{:S(2)}) async-start(f32[128,1,1280]{2,1,0:T(1,128)} %get-tuple-element.7), calls=%async_computation.1 | async-start | bytes 1310720 | tf_op jit(solution)/shard_map/all_to_all | solution.py:290
  139.4 24.4 %all-to-all-start.4 = ((f32[32,1,5120]{2,1,0:T(1,128)}), f32[32,1,5120]{2,1,0:T(1,128)S(1)}, u32[]{:S(2)}, u32[]{:S(2)}) async-start(f32[32,1,5120]{2,1,0:T(1,128)} %analysis.3), calls=%async_computation.4 | async-start | bytes 1310720 | tf_op jit(solution)/shard_map/all_to_all | solution.py:299

commit v3 on v1

--- a/solution.py
+++ b/solution.py
@@ -52,74 +52,123 @@
     return x
 
 
-def forecast_kernel(main_ref, prev_ref, next_ref, mix_ref, rate_ref, out_ref, state, mix, rate):
-    wide = mix_ref[...]
-    high, mid, low = split3(wide)
-    part = lane_index(wide.shape) // PADDED
-    pick_mid = (part == 2) | (part == 3)
-    mix[...] = jnp.where(
-        pick_mid, mid.astype(F32), jnp.where(part == 5, low.astype(F32), high.astype(F32))
-    ).astype(BF16)
-    rate[...] = jnp.broadcast_to(rate_ref[...], (PADDED, GY))
-    pad = jnp.zeros((PADDED - LEVELS, GY), F32)
+def advance(window, mix_ref, rate_ref):
+    centre = window[1:3]
+    high, mid, _ = split3(jnp.concatenate(centre, axis=1))
+    stacked = jnp.concatenate([high, mid, high], axis=0)
+    coupled = jnp.dot(mix_ref[...], stacked, preferred_element_type=F32)
+    result = []
+    for i in range(2):
+        cells = centre[i]
+        around = window[i] + window[i + 2]
+        laplace = around + pltpu.roll(cells, GY - 1, 1) + pltpu.roll(cells, 1, 1) - 4.0 * cells
+        pushed = jnp.tanh(coupled[:, i * GY : (i + 1) * GY])
+        result.append(cells + rate_ref[...] * laplace + 0.3 * pushed)
+    return result
+
+
+def send_rows(results, row, out_ref):
+    for i in range(2):
+        both = jnp.concatenate([results[m][i][0:LEVELS] for m in range(2)], axis=0)
+        moved = swap_blocks(both.reshape(TILES, 8, GY))
+        for tile in range(TILES):
+            out_ref[pl.ds((row + i) * 8, 8), 0, pl.ds(tile * 128, 128)] = moved[tile]
+
+
+def put_row(state_ref, index, cells):
+    state_ref[index + (slice(0, LEVELS), slice(None))] = cells
+    state_ref[index + (slice(LEVELS, PADDED), slice(None))] = jnp.zeros((PADDED - LEVELS, GY), F32)
+
+
+def interior_kernel(main_ref, mix_ref, rate_ref, op_ref, out_ref, edge_ref, mix_out, rate_out, wide_ref, state):
+    table = mix_ref[...]
+    high, mid, _ = split3(table)
+    part = lane_index(table.shape) // PADDED
+    mix_out[...] = jnp.where(part == 2, mid.astype(F32), high.astype(F32)).astype(BF16)
+    rate_out[...] = jnp.broadcast_to(rate_ref[...], (PADDED, GY))
     for m in range(2):
-        for row in range(24):
-            cols = pl.ds((row % 4) * GY, GY)
-            if row < 4:
-                cells = prev_ref[m, :, cols]
-            elif row < 20:
-                cells = main_ref[row // 4 - 1, m, :, cols]
-            else:
-                cells = next_ref[m, :, cols]
-            state[0, m, row, 0:LEVELS, :] = cells
-            state[0, m, row, LEVELS:PADDED, :] = pad
-
-    def advance(now, m, row):
-        centre = [state[now, m, row + i] for i in range(2)]
-        before = state[now, m, row - 1]
-        after = state[now, m, row + 2]
-        parts = split3(jnp.concatenate(centre, axis=1))
-        stacked = jnp.concatenate([parts[i] for i in (0, 1, 0, 1, 2, 0)], axis=0)
-        coupled = jnp.dot(mix[...], stacked, preferred_element_type=F32)
-        result = []
-        for i in range(2):
-            cells = centre[i]
-            around = (centre[1] + before) if i == 0 else (after + centre[0])
-            laplace = (
-                around + pltpu.roll(cells, GY - 1, 1) + pltpu.roll(cells, 1, 1) - 4.0 * cells
-            )
-            pushed = jnp.tanh(coupled[:, i * GY : (i + 1) * GY])
-            result.append(cells + rate[...] * laplace + 0.3 * pushed)
-        return result
-
-    for step in range(NSTEP - 1):
+        for row in range(16):
+            put_row(state, (0, m, row), main_ref[row // 4, m, :, pl.ds((row % 4) * GY, GY)])
+    for step in range(NSTEP):
         now = step % 2
 
         def body(pair, carry, now=now, step=step):
             row = step + 1 + 2 * pair
+            results = [
+                advance([state[now, m, row - 1 + i] for i in range(4)], mix_out, rate_out)
+                for m in range(2)
+            ]
+            if step < NSTEP - 1:
+                for m in range(2):
+                    for i in range(2):
+                        state[1 - now, m, row + i] = results[m][i]
+            else:
+                send_rows(results, row - 4, out_ref)
+            return carry
+
+        lax.fori_loop(0, (14 - 2 * step) // 2, body, 0)
+        if step < NSTEP - 1:
+            done = step + 1
             for m in range(2):
-                result = advance(now, m, row)
-                state[1 - now, m, row] = result[0]
-                state[1 - now, m, row + 1] = result[1]
+                for i, row in enumerate((done, done + 1, 14 - done, 15 - done)):
+                    edge_ref[step, m, i] = state[1 - now, m, row]
+
+    take = lax.broadcasted_iota(jnp.int32, (128, 256), 0)
+    put = lane_index((128, 256))
+    same = (put // 16 == take // 8) & (put % 8 == take % 8)
+    spread = jnp.where(same, 1.0, 0.0).astype(BF16)
+    group = (lane_index((128, 256)) // 8) % 2
+    for j in range(2):
+        for block in range(5):
+            width = 128 if block < 4 else 608 - 512
+            piece = split3(op_ref[j, :, pl.ds(block * 128, width)])
+            grown = [jnp.dot(p, spread[0:width], preferred_element_type=F32) for p in piece]
+            full = (grown[0] + grown[1]) + grown[2]
+            wide_ref[j * 128 : (j + 1) * 128, block * 256 : (block + 1) * 256] = jnp.where(
+                group == j, full, 0.0
+            )
+
+
+def edge_kernel(main_ref, prev_ref, next_ref, inner_ref, edge_ref, mix_ref, rate_ref, out_ref, state):
+    for m in range(2):
+        for i in range(4):
+            cols = pl.ds(i * GY, GY)
+            put_row(state, (0, 0, m, i), prev_ref[m, :, cols])
+            put_row(state, (0, 1, m, 2 + i), next_ref[m, :, cols])
+        for i in range(2):
+            put_row(state, (0, 0, m, 4 + i), main_ref[0, m, :, pl.ds(i * GY, GY)])
+            put_row(state, (0, 1, m, i), main_ref[3, m, :, pl.ds((2 + i) * GY, GY)])
+    for step in range(NSTEP):
+        now = step % 2
+
+        def body(index, carry, now=now, step=step):
+            side, pair = index // 2, index % 2
+            results = [
+                advance([state[now, side, m, 2 * pair + i] for i in range(4)], mix_ref, rate_ref)
+                for m in range(2)
+            ]
+            if step < NSTEP - 1:
+                for m in range(2):
+                    for i in range(2):
+                        state[1 - now, side, m, 2 * side + 2 * pair + i] = results[m][i]
+            else:
+                send_rows(results, 12 * side + 2 * pair, out_ref)
             return carry
 
-        lax.fori_loop(0, (22 - 2 * step) // 2, body, 0)
-
-    def last(pair, carry):
-        row = 4 + 2 * pair
-        results = [advance((NSTEP - 1) % 2, m, row) for m in range(2)]
-        for i in range(2):
-            both = jnp.concatenate([results[m][i][0:LEVELS] for m in range(2)], axis=0)
-            moved = swap_blocks(both.reshape(TILES, 8, GY))
-            start = (2 * pair + i) * 8
-            for tile in range(TILES):
-                out_ref[pl.ds(start, 8), 0, pl.ds(tile * 128, 128)] = moved[tile]
-        return carry
-
-    lax.fori_loop(0, 8, last, 0)
-
-
-def analysis_kernel(x_ref, op_ref, obs_ref, prec_ref, out_ref, pert, wide, yref, rr, zz, ff, moved):
+        lax.fori_loop(0, 4, body, 0)
+        if step < NSTEP - 1:
+            for m in range(2):
+                for i in range(2):
+                    state[1 - now, 0, m, 4 + i] = edge_ref[step, m, i]
+                    state[1 - now, 1, m, i] = edge_ref[step, m, 2 + i]
+
+    for row in range(8):
+        for tile in range(TILES):
+            lanes = pl.ds(tile * 128, 128)
+            out_ref[pl.ds(32 + row * 8, 8), 0, lanes] = inner_ref[pl.ds(row * 8, 8), 0, lanes]
+
+
+def analysis_kernel(x_ref, wide, obs_ref, prec_ref, out_ref, pert, yref, rr, zz, ff, moved):
     low_half = lane_index((128, 128)) < 64
     rows = 128
     for tile in range(10):
@@ -136,23 +185,6 @@
         pert[0:rows, lanes] = even - mean
         pert[rows : 2 * rows, lanes] = odd - mean
         pert[2 * rows : 2 * rows + 8, lanes] = jnp.broadcast_to(mean, (8, 128))
-
-    take = lax.broadcasted_iota(jnp.int32, (128, 256), 0)
-    put = lane_index((128, 256))
-    same = (put // 16 == take // 8) & (put % 8 == take % 8)
-    spread = jnp.where(same, 1.0, 0.0).astype(BF16)
-    group = (lane_index((128, 256)) // 8) % 2
-    for j in range(2):
-        for block in range(5):
-            width = 128 if block < 4 else 608 - 512
-            piece = split3(op_ref[j, :, pl.ds(block * 128, width)])
-            grown = [
-                jnp.dot(p, spread[0:width], preferred_element_type=F32) for p in piece
-            ]
-            full = (grown[0] + grown[1]) + grown[2]
-            wide[j * 128 : (j + 1) * 128, block * 256 : (block + 1) * 256] = jnp.where(
-                group == j, full, 0.0
-            )
 
     yref[...] = lax.dot_general(
         pert[...], wide[...], (((1,), (1,)), ((), ())), precision=HIGHEST, preferred_element_type=F32
@@ -246,18 +278,31 @@
     return pltpu.CompilerParams(vmem_limit_bytes=VMEM_LIMIT)
 
 
-def forecast(main, before, after, mixing, rate):
+def forecast_interior(main, mixing, rate, operator):
     return pl.pallas_call(
-        forecast_kernel,
+        interior_kernel,
+        out_shape=[
+            jax.ShapeDtypeStruct((64, 1, PAIR), F32),
+            jax.ShapeDtypeStruct((NSTEP - 1, 2, 4, PADDED, GY), F32),
+            jax.ShapeDtypeStruct((PADDED, 3 * PADDED), BF16),
+            jax.ShapeDtypeStruct((PADDED, GY), F32),
+            jax.ShapeDtypeStruct((2 * 128, LANES), F32),
+        ],
+        scratch_shapes=[pltpu.VMEM((2, 2, 16, PADDED, GY), F32)],
+        compiler_params=params(),
+        cost_estimate=pl.CostEstimate(flops=10**10, bytes_accessed=8 * 2**20, transcendentals=0),
+        name="interior",
+    )(main, mixing, rate, operator)
+
+
+def forecast_edges(main, before, after, inner, edges, mixing, rate):
+    return pl.pallas_call(
+        edge_kernel,
         out_shape=jax.ShapeDtypeStruct((128, 1, PAIR), F32),
-        scratch_shapes=[
-            pltpu.VMEM((2, 2, 24, PADDED, GY), F32),
-            pltpu.VMEM((PADDED, 6 * PADDED), BF16),
-            pltpu.VMEM((PADDED, GY), F32),
-        ],
+        scratch_shapes=[pltpu.VMEM((2, 2, 2, 6, PADDED, GY), F32)],
         compiler_params=params(),
-        name="forecast",
-    )(main, before, after, mixing, rate)
+        name="edges",
+    )(main, before, after, inner, edges, mixing, rate)
 
 
 def analyse(cells, operator, observed, precisions):
@@ -266,7 +311,6 @@
         out_shape=jax.ShapeDtypeStruct((32, 1, 4 * PAIR), F32),
         scratch_shapes=[
             pltpu.VMEM((MEMBERS + 8, LANES), F32),
-            pltpu.VMEM((2 * 128, LANES), F32),
             pltpu.VMEM((MEMBERS + 8, 2 * 128), F32),
             pltpu.VMEM((2, MEMBERS, MEMBERS), F32),
             pltpu.VMEM((2, MEMBERS, MEMBERS), F32),
@@ -289,7 +333,7 @@
 
 def prepare(blending_matrix, lateral_spreading):
     extra = PADDED - LEVELS
-    mixing = jnp.tile(jnp.pad(blending_matrix, ((0, extra), (0, extra))), (1, 6))
+    mixing = jnp.tile(jnp.pad(blending_matrix, ((0, extra), (0, extra))), (1, 3))
     return mixing, jnp.pad(lateral_spreading, (0, extra))[:, None]
 
 
@@ -299,9 +343,10 @@
     main = lax.all_to_all(split, "x", split_axis=0, concat_axis=0, tiled=True)
     before = lax.ppermute(main[3], "zh", [(i, (i + 1) % 4) for i in range(4)])
     after = lax.ppermute(main[0], "zh", [((i + 1) % 4, i) for i in range(4)])
-    sent = forecast(main, before, after, mixing, rate)
+    inner, edges, mixed, rates, wide = forecast_interior(main, mixing, rate, obs_op)
+    sent = forecast_edges(main, before, after, inner, edges, mixed, rates)
     owned = lax.all_to_all(sent, ("x", "y", "zl", "c"), split_axis=0, concat_axis=0, tiled=True)
-    result = analyse(owned, obs_op, obs_value, obs_precision)
+    result = analyse(owned, wide, obs_value, obs_precision)
     returned = lax.all_to_all(result, ("y", "zl", "c"), split_axis=0, concat_axis=0, tiled=True)
     return restore(returned)
 

time: 193 us -> 189 us (0.979)
  waiting for transfers between devices: 65.1 us -> 27.7 us
  blocking collectives: 53.4 us -> 89.5 us
    all_to_all x1, blocking collectives: 17 us -> 53.2 us  [shards(): lax.all_to_all(sent, ('x', 'y', 'zl', 'c'), split_axis=0, concat_axis=0,...]
    all_to_all x1, waiting for transfers between devices: 33.4 us -> 10.8 us  [shards(): main = lax.all_to_all(split, 'x', split_axis=0, concat_axis=0, tiled=True)]
    ppermute x1, starting transfers between devices: 5.56 us -> 17.4 us  [shards(): after = lax.ppermute(main[0], 'zh', [((i + 1) % 4, i) for i in range(4)])]
    ppermute x1, starting transfers between devices: 12.4 us -> 1.92 us  [shards(): before = lax.ppermute(main[3], 'zh', [(i, (i + 1) % 4) for i in range(4)])]
    ppermute x1, waiting for transfers between devices: 26.2 us -> 16.9 us  [shards(): after = lax.ppermute(main[0], 'zh', [((i + 1) % 4, i) for i in range(4)])]
    ppermute x1, waiting for transfers between devices: 5.46 us -> 0.01 us  [shards(): before = lax.ppermute(main[3], 'zh', [(i, (i + 1) % 4) for i in range(4)])]
    all_to_all x1, starting transfers between devices: 7.61 us -> 4.97 us  [shards(): main = lax.all_to_all(split, 'x', split_axis=0, concat_axis=0, tiled=True)]
    pallas_call x1 -> x2, Pallas kernels: 12.1 us -> 11.1 us  [the longest x1 6.27 us: forecast_interior(): pl.pallas_call(interior_kernel, out_shape=[jax.ShapeDtypeStruct((64, 1, P...]
  transfers between devices with their start and end apart: 3 -> 3, of which waited for: 3 -> 2; matrix products, arithmetic and copies ran while one was open for 0% -> 0% of each run, Pallas kernels for 0% -> 3%
where the time goes in v3:
time: 189 us
  blocking collectives  89.5 us (47%)
  Pallas kernels  41 us (22%)
  waiting for transfers between devices  27.7 us (15%)
  starting transfers between devices  24.2 us (13%)
  local copies, waits for them, and re-layouts  6.61 us (3%)
    all_to_all x1, blocking collectives, shards(): lax.all_to_all(sent, ('x', 'y', 'zl', 'c'), split_axis=0, concat_axis=0,...  53.2 us
    all_to_all x1, blocking collectives, shards(): lax.all_to_all(result, ('y', 'zl', 'c'), split_axis=0, concat_axis=0, til...  36.3 us
    pallas_call x1, Pallas kernels, analyse(): pl.pallas_call(analysis_kernel, out_shape=jax.ShapeDtypeStruct((32, 1, 4...  26.6 us
    ppermute x1, starting transfers between devices, shards(): after = lax.ppermute(main[0], 'zh', [((i + 1) % 4, i) for i in range(4)])  17.4 us
    ppermute x1, waiting for transfers between devices, shards(): after = lax.ppermute(main[0], 'zh', [((i + 1) % 4, i) for i in range(4)])  16.9 us
    all_to_all x1, waiting for transfers between devices, shards(): main = lax.all_to_all(split, 'x', split_axis=0, concat_axis=0, tiled=True)  10.8 us
    pallas_call x1, Pallas kernels, forecast_interior(): pl.pallas_call(interior_kernel, out_shape=[jax.ShapeDtypeStruct((64, 1, P...  6.27 us
    all_to_all x1, starting transfers between devices, shards(): main = lax.all_to_all(split, 'x', split_axis=0, concat_axis=0, tiled=True)  4.97 us
  transfers between devices with their start and end apart: 3, of which 2 were waited for; matrix products, arithmetic and copies ran while one was open for 0% of the time, Pallas kernels for 3%

profile of v3, /device:TPU:1, one launch (start us, length us, event | category | flops | bytes accessed | tf_op | source)
XLA Modules:
  0.0 189.2 jit_solution(16064829995869141962)
XLA Ops:
  0.0 2.0 %copy.26 = f32[8,76,512]{2,1,0:T(8,128)S(1)} copy(f32[8,76,512]{2,0,1:T(8,128)} %param.6) | data formatting | bytes 2490368 | tf_op args[0]
  2.0 2.0 %copy.27 = f32[4,2,76,512]{3,1,2,0:T(2,128)} copy(f32[4,2,76,512]{3,2,1,0:T(8,128)S(1)} %bitcast.8) | data formatting | bytes 2490368 | tf_op jit(solution)/shard_map/reshape | solution.py:342
  4.0 5.0 %all-to-all-start = ((f32[4,2,76,512]{3,1,2,0:T(2,128)}), f32[4,2,76,512]{3,1,2,0:T(2,128)S(1)}, u32[]{:S(2)}, u32[]{:S(2)}) async-start(f32[4,2,76,512]{3,1,2,0:T(2,128)} %copy.27), calls=%async_computation | async-start | bytes 2490368 | tf_op jit(solution)/shard_map/all_to_all | solution.py:343
  9.0 0.0 copy-done.4
  9.0 0.1 copy.33.rate_ref
  9.1 0.0 copy-done.3
  9.1 0.1 copy.37
  9.2 0.1 copy.32.mix_ref
  9.3 0.2 copy.34.op_ref
  9.6 10.8 %all-to-all-done = f32[4,2,76,512]{3,1,2,0:T(2,128)S(1)} async-done(((f32[4,2,76,512]{3,1,2,0:T(2,128)}), f32[4,2,76,512]{3,1,2,0:T(2,128)S(1)}, u32[]{:S(2)}, u32[]{:S(2)}) %all-to-all-start) | async-done | bytes 1245216 | tf_op jit(solution)/shard_map/all_to_all | solution.py:343
  20.4 0.2 copy.35.main_ref
  20.7 17.4 %collective-permute-start.1 = (f32[2,76,512]{2,1,0:T(8,128)S(1)}, f32[2,76,512]{2,1,0:T(8,128)S(1)}, u32[]{:S(2)}, u32[]{:S(2)}) collective-permute-start(f32[2,76,512]{2,1,0:T(8,128)S(1)} %get-tuple-element.15), channel_id=1, source_target_pairs={{4,0},{8,4},{12,8},{0,12},{5,1},{9,5},{13,9},{1,13},{6,2},{10,6},{... | collective-permute-start | bytes 933896 | tf_op jit(solution)/shard_map/ppermute | solution.py:345
  38.0 1.9 %collective-permute-start = (f32[2,76,512]{2,1,0:T(8,128)S(1)}, f32[2,76,512]{2,1,0:T(8,128)S(1)}, u32[]{:S(2)}, u32[]{:S(2)}) collective-permute-start(f32[2,76,512]{2,1,0:T(8,128)S(1)} %get-tuple-element.16), channel_id=1, source_target_pairs={{0,4},{4,8},{8,12},{12,0},{1,5},{5,9},{9,13},{13,1},{2,6},{6,10},{... | collective-permute-start | bytes 933896 | tf_op jit(solution)/shard_map/ppermute | solution.py:344
  40.0 6.3 %interior.1 = (f32[64,1,2432]{2,1,0:T(1,128)S(1)}, f32[3,2,4,80,128]{4,3,2,1,0:T(8,128)S(1)}, bf16[80,240]{1,0:T(8,128)(2,1)S(1)}, f32[80,128]{1,0:T(8,128)S(1)}, f32[256,1280]{1,0:T(8,128)S(1)}) custom-call(f32[4,2,76,512]{3,2,1,0:T(8,128)S(1)} %copy.35.main_ref, f32[80,240]{1,0:T(8,128)S(1)} %copy.32.mix_ref, f32[80,1]{1,0:T(8,128)S(1)} %copy.33.rate_ref, ...), custom_call_target="tpu_custom_call" | custom-call | flops 10000000000 | bytes 8388608 | tf_op jit(solution)/shard_map/interior/pallas_call | solution.py:282
  46.3 16.9 %collective-permute-done.1.next_ref = f32[2,76,512]{2,1,0:T(8,128)S(1)} collective-permute-done((f32[2,76,512]{2,1,0:T(8,128)S(1)}, f32[2,76,512]{2,1,0:T(8,128)S(1)}, u32[]{:S(2)}, u32[]{:S(2)}) %collective-permute-start.1) | collective-permute-done | bytes 311328 | tf_op jit(solution)/shard_map/ppermute | solution.py:345
  63.2 0.0 collective-permute-done.prev_ref
  63.2 4.9 %edges.1 = f32[128,1,2432]{2,1,0:T(1,128)S(1)} custom-call(f32[4,2,76,512]{3,2,1,0:T(8,128)S(1)} %copy.35.main_ref, f32[2,76,512]{2,1,0:T(8,128)S(1)} %collective-permute-done.prev_ref, f32[2,76,512]{2,1,0:T(8,128)S(1)} %collective-permute-done.1.next_ref, f32[64,1,2432]{2,1,0:T(1,128)S(1)} %get-tuple-element.10.inner_ref, ...), custom_call_target="tpu_custom_call" | custom-call | tf_op jit(solution)/shard_map/edges/pallas_call | solution.py:299
  68.0 0.0 copy-start
  68.1 0.0 copy-start.1
  68.1 53.2 %all_to_all.15.x_ref = f32[128,1,2432]{2,1,0:T(1,128)S(1)} all-to-all(f32[128,1,2432]{2,1,0:T(1,128)S(1)} %edges.1), channel_id=1, replica_groups=mesh['y'=4,'zl'=4,'c'=2,'zh'=4,'x'=4] {'x','y','zl','c'}, dimensions={0} | all-to-all | bytes 2490368 | tf_op jit(solution)/shard_map/all_to_all | solution.py:348
  121.3 26.6 %analysis.1 = f32[32,1,9728]{2,1,0:T(1,128)S(1)} custom-call(f32[128,1,2432]{2,1,0:T(1,128)S(1)} %all_to_all.15.x_ref, f32[256,1280]{1,0:T(8,128)S(1)} %get-tuple-element.14.wide, f32[2,128]{1,0:T(2,128)S(1)} %copy-done, f32[2,128]{1,0:T(2,128)S(1)} %copy-done.1), custom_call_target="tpu_custom_call" | custom-call | tf_op jit(solution)/shard_map/analysis/pallas_call | solution.py:309
  147.9 36.3 %all_to_all.16.in_ref = f32[32,1,9728]{2,1,0:T(1,128)S(1)} all-to-all(f32[32,1,9728]{2,1,0:T(1,128)S(1)} %analysis.1), channel_id=1, replica_groups=mesh['y'=4,'zl'=4,'c'=2,'zh'=4,'x'=4] {'y','zl','c'}, dimensions={0} | all-to-all | bytes 2490368 | tf_op jit(solution)/shard_map/all_to_all | solution.py:350
  184.2 3.2 %restore.1 = f32[8,76,512]{2,1,0:T(8,128)S(1)} custom-call(f32[32,1,9728]{2,1,0:T(1,128)S(1)} %all_to_all.16.in_ref), custom_call_target="tpu_custom_call" | custom-call | tf_op jit(solution)/shard_map/restore/pallas_call | solution.py:326
  187.4 1.8 copy.36
  (10 shorter events, 0.1 us)
Async XLA Ops:
  4.0 5.0 %copy-start.4 = (f32[76]{0:T(128)S(1)}, f32[76]{0:T(128)}, u32[]{:S(2)}) copy-start(f32[76]{0:T(128)} %param.8) | copy-start | bytes 916
  4.0 5.1 %copy-start.3 = (f32[76,76]{1,0:T(8,128)S(1)}, f32[76,76]{1,0:T(8,128)}, u32[]{:S(2)}) copy-start(f32[76,76]{1,0:T(8,128)} %param.7) | copy-start | bytes 69316
  4.0 5.3 %copy-start.2 = (f32[2,128,608]{1,2,0:T(8,128)S(1)}, f32[2,128,608]{1,2,0:T(8,128)}, u32[]{:S(2)}) copy-start(f32[2,128,608]{1,2,0:T(8,128)} %param.9) | copy-start | bytes 1867780
  4.0 16.4 %all-to-all-start = ((f32[4,2,76,512]{3,1,2,0:T(2,128)}), f32[4,2,76,512]{3,1,2,0:T(2,128)S(1)}, u32[]{:S(2)}, u32[]{:S(2)}) async-start(f32[4,2,76,512]{3,1,2,0:T(2,128)} %copy.27), calls=%async_computation | async-start | bytes 2490368 | tf_op jit(solution)/shard_map/all_to_all | solution.py:343
  20.7 42.5 %collective-permute-start.1 = (f32[2,76,512]{2,1,0:T(8,128)S(1)}, f32[2,76,512]{2,1,0:T(8,128)S(1)}, u32[]{:S(2)}, u32[]{:S(2)}) collective-permute-start(f32[2,76,512]{2,1,0:T(8,128)S(1)} %get-tuple-element.15), channel_id=1, source_target_pairs={{4,0},{8,4},{12,8},{0,12},{5,1},{9,5},{13,9},{1,13},{6,2},{10,6},{... | collective-permute-start | bytes 933896 | tf_op jit(solution)/shard_map/ppermute | solution.py:345
  38.0 25.1 %collective-permute-start = (f32[2,76,512]{2,1,0:T(8,128)S(1)}, f32[2,76,512]{2,1,0:T(8,128)S(1)}, u32[]{:S(2)}, u32[]{:S(2)}) collective-permute-start(f32[2,76,512]{2,1,0:T(8,128)S(1)} %get-tuple-element.16), channel_id=1, source_target_pairs={{0,4},{4,8},{8,12},{12,0},{1,5},{5,9},{9,13},{13,1},{2,6},{6,10},{... | collective-permute-start | bytes 933896 | tf_op jit(solution)/shard_map/ppermute | solution.py:344
  68.0 53.2 %copy-start = (f32[2,128]{1,0:T(2,128)S(1)}, f32[2,128]{1,0:T(2,128)}, u32[]{:S(2)}) copy-start(f32[2,128]{1,0:T(2,128)} %obs_ref.1) | copy-start | bytes 3076
  68.1 53.2 %copy-start.1 = (f32[2,128]{1,0:T(2,128)S(1)}, f32[2,128]{1,0:T(2,128)}, u32[]{:S(2)}) copy-start(f32[2,128]{1,0:T(2,128)} %prec_ref.1) | copy-start | bytes 3076

commit v4 on v3

--- a/solution.py
+++ b/solution.py
@@ -80,6 +80,11 @@
     state_ref[index + (slice(LEVELS, PADDED), slice(None))] = jnp.zeros((PADDED - LEVELS, GY), F32)
 
 
+def deal_kernel(in_ref, out_ref):
+    for x in range(4):
+        out_ref[x] = in_ref[:, 2 * x : 2 * x + 2, :]
+
+
 def interior_kernel(main_ref, mix_ref, rate_ref, op_ref, out_ref, edge_ref, mix_out, rate_out, wide_ref, state):
     table = mix_ref[...]
     high, mid, _ = split3(table)
@@ -88,7 +93,7 @@
     rate_out[...] = jnp.broadcast_to(rate_ref[...], (PADDED, GY))
     for m in range(2):
         for row in range(16):
-            put_row(state, (0, m, row), main_ref[row // 4, m, :, pl.ds((row % 4) * GY, GY)])
+            put_row(state, (0, m, row), main_ref[row // 4, :, m, pl.ds((row % 4) * GY, GY)])
     for step in range(NSTEP):
         now = step % 2
 
@@ -133,11 +138,11 @@
     for m in range(2):
         for i in range(4):
             cols = pl.ds(i * GY, GY)
-            put_row(state, (0, 0, m, i), prev_ref[m, :, cols])
-            put_row(state, (0, 1, m, 2 + i), next_ref[m, :, cols])
+            put_row(state, (0, 0, m, i), prev_ref[:, m, cols])
+            put_row(state, (0, 1, m, 2 + i), next_ref[:, m, cols])
         for i in range(2):
-            put_row(state, (0, 0, m, 4 + i), main_ref[0, m, :, pl.ds(i * GY, GY)])
-            put_row(state, (0, 1, m, i), main_ref[3, m, :, pl.ds((2 + i) * GY, GY)])
+            put_row(state, (0, 0, m, 4 + i), main_ref[0, :, m, pl.ds(i * GY, GY)])
+            put_row(state, (0, 1, m, i), main_ref[3, :, m, pl.ds((2 + i) * GY, GY)])
     for step in range(NSTEP):
         now = step % 2
 
@@ -168,7 +173,7 @@
             out_ref[pl.ds(32 + row * 8, 8), 0, lanes] = inner_ref[pl.ds(row * 8, 8), 0, lanes]
 
 
-def analysis_kernel(x_ref, wide, obs_ref, prec_ref, out_ref, pert, yref, rr, zz, ff, moved):
+def analysis_kernel(x_ref, wide, obs_ref, prec_ref, out_ref, pert, yref, rr, zz, ff, moved, roots):
     low_half = lane_index((128, 128)) < 64
     rows = 128
     for tile in range(10):
@@ -233,42 +238,44 @@
         pull = jnp.sum(y * prec_ref[j : j + 1, :] * innovation, axis=1, keepdims=True)
         half = jnp.sum(root * pull, axis=0, keepdims=True)
         weight = jnp.sum(root * half, axis=1, keepdims=True)
-        zz[j] = math.sqrt(MEMBERS - 1.0) * root
         shifts.append(weight)
+        for i, part in enumerate(split3(math.sqrt(MEMBERS - 1.0) * root)[0:2]):
+            roots[i, j] = part
     for block in range(5):
         lanes = pl.ds(block * 256, 256)
         own = (lane_index((MEMBERS, 256)) // 8) % 2 == 0
         cells = pert[0:MEMBERS, lanes]
+        high, mid, _ = split3(cells)
         terms = []
         for j in range(2):
             base = pert[MEMBERS : MEMBERS + 1, lanes] + jnp.sum(cells * shifts[j], axis=0, keepdims=True)
-            terms.append(base + mm(zz[j], cells))
+            small = jnp.dot(roots[0, j], mid, preferred_element_type=F32) + jnp.dot(
+                roots[1, j], high, preferred_element_type=F32
+            )
+            terms.append(base + (jnp.dot(roots[0, j], high, preferred_element_type=F32) + small))
         moved[:, lanes] = jnp.where(own, terms[0], terms[1])
-    for tile in range(TILES):
-        if tile < 9:
-            value = moved[0:rows, tile * 128 : (tile + 1) * 128]
-        elif tile == 9:
-            rolled = pltpu.roll(moved[rows : 2 * rows, 0:128], 64, 1)
-            value = jnp.where(low_half, moved[0:rows, 9 * 128 : 10 * 128], rolled)
-        else:
-            i = tile - 10
-            first = moved[rows : 2 * rows, i * 128 : (i + 1) * 128]
-            second = moved[rows : 2 * rows, (i + 1) * 128 : (i + 2) * 128]
-            value = pltpu.roll(jnp.where(low_half, second, first), 64, 1)
-        for s in range(4):
-            out_ref[:, 0, pl.ds(s * PAIR + tile * 128, 128)] = value[s * 32 : (s + 1) * 32]
+    lane_block = lane_index((32, 128)) // 16
+    for tile in range(10):
+        cols = pl.ds(tile * 128, 128)
+        group = [moved[(m % 2) * rows + (m // 2) * 32 : (m % 2) * rows + (m // 2) * 32 + 32, cols] for m in range(8)]
+        for bit in (1, 2, 4):
+            up = (lane_block & bit) != 0
+            for m in range(8):
+                if m & bit:
+                    continue
+                low, high = group[m], group[m | bit]
+                group[m] = jnp.where(up, pltpu.roll(high, 16 * bit, 1), low)
+                group[m | bit] = jnp.where(up, high, pltpu.roll(low, 128 - 16 * bit, 1))
+        for i in range(8 if tile < 9 else 4):
+            out_ref[:, 0, pl.ds((tile * 8 + i) * 128, 128)] = group[i]
 
 
 def restore_kernel(in_ref, out_ref):
-    def body(s, carry):
-        for y in range(4):
-            tiles = [
-                in_ref[pl.ds(y * 8, 8), 0, pl.ds(pl.multiple_of(s * PAIR + tile * 128, 128), 128)]
-                for tile in range(TILES)
-            ]
-            moved = swap_blocks(jnp.stack(tiles, axis=0)).reshape(2 * LEVELS, GY)
-            out_ref[2 * s, :, y * GY : (y + 1) * GY] = moved[0:LEVELS]
-            out_ref[2 * s + 1, :, y * GY : (y + 1) * GY] = moved[LEVELS : 2 * LEVELS]
+    def body(y, carry):
+        cols = pl.ds(pl.multiple_of(y * GY, GY), GY)
+        for first in range(0, LEVELS, 19):
+            tiles = [in_ref[pl.ds(y * 8, 8), 0, pl.ds((first + i) * 128, 128)] for i in range(19)]
+            out_ref[first : first + 19, :, cols] = swap_blocks(jnp.stack(tiles, axis=0))
         return carry
 
     lax.fori_loop(0, 4, body, 0)
@@ -276,6 +283,15 @@
 
 def params():
     return pltpu.CompilerParams(vmem_limit_bytes=VMEM_LIMIT)
+
+
+def deal(cells):
+    return pl.pallas_call(
+        deal_kernel,
+        out_shape=jax.ShapeDtypeStruct((4, LEVELS, 2, 4 * GY), F32),
+        compiler_params=params(),
+        name="deal",
+    )(cells)
 
 
 def forecast_interior(main, mixing, rate, operator):
@@ -316,6 +332,7 @@
             pltpu.VMEM((2, MEMBERS, MEMBERS), F32),
             pltpu.VMEM((2, MEMBERS, MEMBERS), F32),
             pltpu.VMEM((MEMBERS, LANES), F32),
+            pltpu.VMEM((2, 2, MEMBERS, MEMBERS), BF16),
         ],
         compiler_params=params(),
         name="analysis",
@@ -325,7 +342,7 @@
 def restore(cells):
     return pl.pallas_call(
         restore_kernel,
-        out_shape=jax.ShapeDtypeStruct((8, LEVELS, 4 * GY), F32),
+        out_shape=jax.ShapeDtypeStruct((LEVELS, 8, 4 * GY), F32),
         compiler_params=params(),
         name="restore",
     )(cells)
@@ -339,7 +356,7 @@
 
 def shards(ensemble, blending_matrix, lateral_spreading, obs_op, obs_value, obs_precision):
     mixing, rate = prepare(blending_matrix, lateral_spreading)
-    split = ensemble.reshape(4, 2, LEVELS, 4 * GY)
+    split = deal(ensemble.transpose(1, 0, 2))
     main = lax.all_to_all(split, "x", split_axis=0, concat_axis=0, tiled=True)
     before = lax.ppermute(main[3], "zh", [(i, (i + 1) % 4) for i in range(4)])
     after = lax.ppermute(main[0], "zh", [((i + 1) % 4, i) for i in range(4)])
@@ -348,7 +365,7 @@
     owned = lax.all_to_all(sent, ("x", "y", "zl", "c"), split_axis=0, concat_axis=0, tiled=True)
     result = analyse(owned, wide, obs_value, obs_precision)
     returned = lax.all_to_all(result, ("y", "zl", "c"), split_axis=0, concat_axis=0, tiled=True)
-    return restore(returned)
+    return restore(returned).transpose(1, 0, 2)
 
 
 def solution(mesh):

time: 189 us -> 186 us (0.984)
  local copies, waits for them, and re-layouts: 6.61 us -> 2.06 us
  Pallas kernels: 41 us -> 43.9 us
  waiting for transfers between devices: 27.7 us -> 25.6 us
    pallas_call x1 -> x2, Pallas kernels: 3.24 us -> 5.6 us  [the longest x1 4.32 us: restore(): pl.pallas_call(restore_kernel, out_shape=jax.ShapeDtypeStruct((LEVELS, 8,...]
    ppermute x1, waiting for transfers between devices: 16.9 us -> 14.8 us  [shards(): after = lax.ppermute(main[0], 'zh', [((i + 1) % 4, i) for i in range(4)])]
    reshape x1 -> x0, local copies, waits for them, and re-layouts: 2 us -> none  [shards(): split = ensemble.reshape(4, 2, LEVELS, 4 * GY)]
  transfers between devices with their start and end apart: 3 -> 3, of which waited for: 2 -> 2; matrix products, arithmetic and copies ran while one was open for 0% -> 0% of each run, Pallas kernels for 3% -> 4%
where the time goes in v4:
time: 186 us; the launch traced here: 185 us
  blocking collectives  89.3 us (48%)
  Pallas kernels  43.9 us (24%)
  waiting for transfers between devices  25.6 us (14%)
  starting transfers between devices  24.2 us (13%)
  local copies, waits for them, and re-layouts  2.06 us (1%)
    all_to_all x1, blocking collectives, shards(): lax.all_to_all(sent, ('x', 'y', 'zl', 'c'), split_axis=0, concat_axis=0,...  52.9 us
    all_to_all x1, blocking collectives, shards(): lax.all_to_all(result, ('y', 'zl', 'c'), split_axis=0, concat_axis=0, til...  36.3 us
    pallas_call x1, Pallas kernels, analyse(): pl.pallas_call(analysis_kernel, out_shape=jax.ShapeDtypeStruct((32, 1, 4...  25.6 us
    ppermute x1, starting transfers between devices, shards(): after = lax.ppermute(main[0], 'zh', [((i + 1) % 4, i) for i in range(4)])  17.4 us
    ppermute x1, waiting for transfers between devices, shards(): after = lax.ppermute(main[0], 'zh', [((i + 1) % 4, i) for i in range(4)])  14.8 us
    all_to_all x1, waiting for transfers between devices, shards(): main = lax.all_to_all(split, 'x', split_axis=0, concat_axis=0, tiled=True)  10.8 us
    pallas_call x1, Pallas kernels, forecast_interior(): pl.pallas_call(interior_kernel, out_shape=[jax.ShapeDtypeStruct((64, 1, P...  7.18 us
    pallas_call x1, Pallas kernels, forecast_edges(): pl.pallas_call(edge_kernel, out_shape=jax.ShapeDtypeStruct((128, 1, PAIR)...  5.57 us
  transfers between devices with their start and end apart: 3, of which 2 were waited for; matrix products, arithmetic and copies ran while one was open for 0% of the time, Pallas kernels for 4%

profile of v4, /device:TPU:1, one launch (start us, length us, event | category | flops | bytes accessed | tf_op | source)
XLA Modules:
  0.0 185.3 jit_solution(728137518788245953)
XLA Ops:
  0.0 1.3 copy-done
  1.3 1.3 deal.1
  2.6 5.0 %all-to-all-start = ((f32[4,76,2,512]{3,2,1,0:T(2,128)}), f32[4,76,2,512]{3,2,1,0:T(2,128)S(1)}, u32[]{:S(2)}, u32[]{:S(2)}) async-start(f32[4,76,2,512]{3,2,1,0:T(2,128)} %deal.1), calls=%async_computation | async-start | bytes 2490368 | tf_op jit(solution)/shard_map/all_to_all | solution.py:360
  7.6 0.0 copy-done.5
  7.6 0.1 copy.11.rate_ref
  7.7 0.0 copy-done.4
  7.7 0.1 copy.13
  7.8 0.1 copy.10.mix_ref
  7.9 0.2 copy.12.op_ref
  8.1 10.8 %all-to-all-done.main_ref = f32[4,76,2,512]{3,2,1,0:T(2,128)S(1)} async-done(((f32[4,76,2,512]{3,2,1,0:T(2,128)}), f32[4,76,2,512]{3,2,1,0:T(2,128)S(1)}, u32[]{:S(2)}, u32[]{:S(2)}) %all-to-all-start) | async-done | bytes 1245216 | tf_op jit(solution)/shard_map/all_to_all | solution.py:360
  18.9 0.2 slice_bitcast_fusion
  19.2 17.4 %collective-permute-start.1 = (f32[76,2,512]{2,1,0:T(2,128)S(1)}, f32[76,2,512]{2,1,0:T(2,128)S(1)}, u32[]{:S(2)}, u32[]{:S(2)}) collective-permute-start(f32[76,2,512]{2,1,0:T(2,128)S(1)} %get-tuple-element.15), channel_id=1, source_target_pairs={{4,0},{8,4},{12,8},{0,12},{5,1},{9,5},{13,9},{1,13},{6,2},{10,6},{... | collective-permute-start | bytes 933896 | tf_op jit(solution)/shard_map/ppermute | solution.py:362
  36.5 1.9 %collective-permute-start = (f32[76,2,512]{2,1,0:T(2,128)S(1)}, f32[76,2,512]{2,1,0:T(2,128)S(1)}, u32[]{:S(2)}, u32[]{:S(2)}) collective-permute-start(f32[76,2,512]{2,1,0:T(2,128)S(1)} %get-tuple-element.16), channel_id=1, source_target_pairs={{0,4},{4,8},{8,12},{12,0},{1,5},{5,9},{9,13},{13,1},{2,6},{6,10},{... | collective-permute-start | bytes 933896 | tf_op jit(solution)/shard_map/ppermute | solution.py:361
  38.5 7.2 %interior.1 = (f32[64,1,2432]{2,1,0:T(1,128)S(1)}, f32[3,2,4,80,128]{4,3,2,1,0:T(8,128)S(1)}, bf16[80,240]{1,0:T(8,128)(2,1)S(1)}, f32[80,128]{1,0:T(8,128)S(1)}, f32[256,1280]{1,0:T(8,128)S(1)}) custom-call(f32[4,76,2,512]{3,2,1,0:T(2,128)S(1)} %all-to-all-done.main_ref, f32[80,240]{1,0:T(8,128)S(1)} %copy.10.mix_ref, f32[80,1]{1,0:T(8,128)S(1)} %copy.11.rate_ref, ...), custom_call_target="tpu_custom_call" | custom-call | flops 10000000000 | bytes 8388608 | tf_op jit(solution)/shard_map/interior/pallas_call | solution.py:298
  45.6 14.8 %collective-permute-done.1.next_ref = f32[76,2,512]{2,1,0:T(2,128)S(1)} collective-permute-done((f32[76,2,512]{2,1,0:T(2,128)S(1)}, f32[76,2,512]{2,1,0:T(2,128)S(1)}, u32[]{:S(2)}, u32[]{:S(2)}) %collective-permute-start.1) | collective-permute-done | bytes 311328 | tf_op jit(solution)/shard_map/ppermute | solution.py:362
  60.5 0.0 collective-permute-done.prev_ref
  60.5 5.6 %edges.1 = f32[128,1,2432]{2,1,0:T(1,128)S(1)} custom-call(f32[4,76,2,512]{3,2,1,0:T(2,128)S(1)} %all-to-all-done.main_ref, f32[76,2,512]{2,1,0:T(2,128)S(1)} %collective-permute-done.prev_ref, f32[76,2,512]{2,1,0:T(2,128)S(1)} %collective-permute-done.1.next_ref, f32[64,1,2432]{2,1,0:T(1,128)S(1)} %get-tuple-element.10.inner_ref, ...), custom_call_target="tpu_custom_call" | custom-call | tf_op jit(solution)/shard_map/edges/pallas_call | solution.py:315
  66.0 0.0 copy-start.1
  66.1 0.0 copy-start.2
  66.1 52.9 %all_to_all.15.x_ref = f32[128,1,2432]{2,1,0:T(1,128)S(1)} all-to-all(f32[128,1,2432]{2,1,0:T(1,128)S(1)} %edges.1), channel_id=1, replica_groups=mesh['y'=4,'zl'=4,'c'=2,'zh'=4,'x'=4] {'x','y','zl','c'}, dimensions={0} | all-to-all | bytes 2490368 | tf_op jit(solution)/shard_map/all_to_all | solution.py:365
  119.0 0.0 copy-done.2
  119.0 25.6 %analysis.1 = f32[32,1,9728]{2,1,0:T(1,128)S(1)} custom-call(f32[128,1,2432]{2,1,0:T(1,128)S(1)} %all_to_all.15.x_ref, f32[256,1280]{1,0:T(8,128)S(1)} %get-tuple-element.14.wide, f32[2,128]{1,0:T(2,128)S(1)} %copy-done.1, f32[2,128]{1,0:T(2,128)S(1)} %copy-done.2), custom_call_target="tpu_custom_call" | custom-call | tf_op jit(solution)/shard_map/analysis/pallas_call | solution.py:325
  144.6 36.3 %all_to_all.16.in_ref = f32[32,1,9728]{2,1,0:T(1,128)S(1)} all-to-all(f32[32,1,9728]{2,1,0:T(1,128)S(1)} %analysis.1), channel_id=1, replica_groups=mesh['y'=4,'zl'=4,'c'=2,'zh'=4,'x'=4] {'y','zl','c'}, dimensions={0} | all-to-all | bytes 2490368 | tf_op jit(solution)/shard_map/all_to_all | solution.py:367
  180.9 4.3 %restore.1 = f32[76,8,512]{2,1,0:T(8,128)} custom-call(f32[32,1,9728]{2,1,0:T(1,128)S(1)} %all_to_all.16.in_ref), custom_call_target="tpu_custom_call" | custom-call | tf_op jit(solution)/shard_map/restore/pallas_call | solution.py:343
  (9 shorter events, 0.0 us)
Async XLA Ops:
  0.0 1.3 copy-start
  2.6 5.0 %copy-start.5 = (f32[76]{0:T(128)S(1)}, f32[76]{0:T(128)}, u32[]{:S(2)}) copy-start(f32[76]{0:T(128)} %param.8) | copy-start | bytes 916
  2.6 5.1 %copy-start.4 = (f32[76,76]{1,0:T(8,128)S(1)}, f32[76,76]{1,0:T(8,128)}, u32[]{:S(2)}) copy-start(f32[76,76]{1,0:T(8,128)} %param.7) | copy-start | bytes 69316
  2.6 5.3 %copy-start.3 = (f32[2,128,608]{1,2,0:T(8,128)S(1)}, f32[2,128,608]{1,2,0:T(8,128)}, u32[]{:S(2)}) copy-start(f32[2,128,608]{1,2,0:T(8,128)} %param.9) | copy-start | bytes 1867780
  2.6 16.4 %all-to-all-start = ((f32[4,76,2,512]{3,2,1,0:T(2,128)}), f32[4,76,2,512]{3,2,1,0:T(2,128)S(1)}, u32[]{:S(2)}, u32[]{:S(2)}) async-start(f32[4,76,2,512]{3,2,1,0:T(2,128)} %deal.1), calls=%async_computation | async-start | bytes 2490368 | tf_op jit(solution)/shard_map/all_to_all | solution.py:360
  19.2 41.3 %collective-permute-start.1 = (f32[76,2,512]{2,1,0:T(2,128)S(1)}, f32[76,2,512]{2,1,0:T(2,128)S(1)}, u32[]{:S(2)}, u32[]{:S(2)}) collective-permute-start(f32[76,2,512]{2,1,0:T(2,128)S(1)} %get-tuple-element.15), channel_id=1, source_target_pairs={{4,0},{8,4},{12,8},{0,12},{5,1},{9,5},{13,9},{1,13},{6,2},{10,6},{... | collective-permute-start | bytes 933896 | tf_op jit(solution)/shard_map/ppermute | solution.py:362
  36.5 23.9 %collective-permute-start = (f32[76,2,512]{2,1,0:T(2,128)S(1)}, f32[76,2,512]{2,1,0:T(2,128)S(1)}, u32[]{:S(2)}, u32[]{:S(2)}) collective-permute-start(f32[76,2,512]{2,1,0:T(2,128)S(1)} %get-tuple-element.16), channel_id=1, source_target_pairs={{0,4},{4,8},{8,12},{12,0},{1,5},{5,9},{9,13},{13,1},{2,6},{6,10},{... | collective-permute-start | bytes 933896 | tf_op jit(solution)/shard_map/ppermute | solution.py:361
  66.0 53.0 %copy-start.1 = (f32[2,128]{1,0:T(2,128)S(1)}, f32[2,128]{1,0:T(2,128)}, u32[]{:S(2)}) copy-start(f32[2,128]{1,0:T(2,128)} %obs_ref.1) | copy-start | bytes 3076
  66.1 53.0 %copy-start.2 = (f32[2,128]{1,0:T(2,128)S(1)}, f32[2,128]{1,0:T(2,128)}, u32[]{:S(2)}) copy-start(f32[2,128]{1,0:T(2,128)} %prec_ref.1) | copy-start | bytes 3076

commit v5 on v4

--- a/solution.py
+++ b/solution.py
@@ -134,7 +134,9 @@
             )
 
 
-def edge_kernel(main_ref, prev_ref, next_ref, inner_ref, edge_ref, mix_ref, rate_ref, out_ref, state):
+def edge_kernel(main_ref, next_ref, prev_ref, inner_ref, edge_ref, mix_ref, rate_ref, out_ref, state, sem):
+    inner = pltpu.make_async_copy(inner_ref, out_ref.at[pl.ds(32, 64)], sem)
+    inner.start()
     for m in range(2):
         for i in range(4):
             cols = pl.ds(i * GY, GY)
@@ -167,13 +169,10 @@
                     state[1 - now, 0, m, 4 + i] = edge_ref[step, m, i]
                     state[1 - now, 1, m, i] = edge_ref[step, m, 2 + i]
 
-    for row in range(8):
-        for tile in range(TILES):
-            lanes = pl.ds(tile * 128, 128)
-            out_ref[pl.ds(32 + row * 8, 8), 0, lanes] = inner_ref[pl.ds(row * 8, 8), 0, lanes]
-
-
-def analysis_kernel(x_ref, wide, obs_ref, prec_ref, out_ref, pert, yref, rr, zz, ff, moved, roots):
+    inner.wait()
+
+
+def analysis_kernel(x_ref, wide, obs_ref, prec_ref, out_ref, pert, yref, moved, roots, *parts):
     low_half = lane_index((128, 128)) < 64
     rows = 128
     for tile in range(10):
@@ -201,6 +200,18 @@
     def mm(a, b):
         return jnp.dot(a, b, precision=HIGHEST, preferred_element_type=F32)
 
+    def put(refs, x):
+        for ref, part in zip(refs, split3(x)):
+            ref[...] = part
+
+    def product(a, b):
+        total = None
+        for i, k in ((2, 0), (0, 2), (1, 1), (1, 0), (0, 1), (0, 0)):
+            term = jnp.dot(a[i][...], b[k][...], preferred_element_type=F32)
+            total = term if total is None else term + total
+        return total
+
+    rr, zz, ff = [[parts[9 * j + 3 * i : 9 * j + 3 * i + 3] for j in range(2)] for i in range(3)]
     scale = []
     for j in range(2):
         obs = slice(j * 128, (j + 1) * 128)
@@ -214,24 +225,29 @@
         scale.append(norm)
         start = system / norm
         factor = 0.5 * (3.0 * eye - start)
-        ff[j] = start
-        zz[j] = factor
-        rr[j] = mm(start, factor)
+        put(zz[j], factor)
+        put(rr[j], mm(start, factor))
+
+    def newton(last=False):
+        for j in range(2):
+            put(ff[j], 0.5 * (3.0 * eye - product(zz[j], rr[j])))
+        if last:
+            return [product(ff[j], zz[j]) for j in range(2)]
+        for j in range(2):
+            put(rr[j], product(rr[j], ff[j]))
+        for j in range(2):
+            put(zz[j], product(ff[j], zz[j]))
+        return None
 
     def body(step, carry):
-        for j in range(2):
-            ff[j] = 0.5 * (3.0 * eye - mm(zz[j], rr[j]))
-        for j in range(2):
-            rr[j] = mm(rr[j], ff[j])
-        for j in range(2):
-            zz[j] = mm(ff[j], zz[j])
+        newton()
         return carry
 
     lax.fori_loop(0, ITERS - 2, body, 0)
+    ends = newton(last=True)
     shifts = []
     for j in range(2):
-        factor = 0.5 * (3.0 * eye - mm(zz[j], rr[j]))
-        root = mm(factor, zz[j]) / jnp.sqrt(scale[j])
+        root = ends[j] / jnp.sqrt(scale[j])
         obs = slice(j * 128, (j + 1) * 128)
         y = yref[0:MEMBERS, obs]
         innovation = obs_ref[j : j + 1, :] - yref[MEMBERS : MEMBERS + 1, obs]
@@ -271,14 +287,9 @@
 
 
 def restore_kernel(in_ref, out_ref):
-    def body(y, carry):
-        cols = pl.ds(pl.multiple_of(y * GY, GY), GY)
-        for first in range(0, LEVELS, 19):
-            tiles = [in_ref[pl.ds(y * 8, 8), 0, pl.ds((first + i) * 128, 128)] for i in range(19)]
-            out_ref[first : first + 19, :, cols] = swap_blocks(jnp.stack(tiles, axis=0))
-        return carry
-
-    lax.fori_loop(0, 4, body, 0)
+    for first in range(0, LEVELS, 19):
+        tiles = [in_ref[:, 0, pl.ds((first + i) * 128, 128)] for i in range(19)]
+        out_ref[first : first + 19] = swap_blocks(jnp.stack(tiles, axis=0))
 
 
 def params():
@@ -315,10 +326,10 @@
     return pl.pallas_call(
         edge_kernel,
         out_shape=jax.ShapeDtypeStruct((128, 1, PAIR), F32),
-        scratch_shapes=[pltpu.VMEM((2, 2, 2, 6, PADDED, GY), F32)],
+        scratch_shapes=[pltpu.VMEM((2, 2, 2, 6, PADDED, GY), F32), pltpu.SemaphoreType.DMA],
         compiler_params=params(),
         name="edges",
-    )(main, before, after, inner, edges, mixing, rate)
+    )(main, after, before, inner, edges, mixing, rate)
 
 
 def analyse(cells, operator, observed, precisions):
@@ -328,11 +339,9 @@
         scratch_shapes=[
             pltpu.VMEM((MEMBERS + 8, LANES), F32),
             pltpu.VMEM((MEMBERS + 8, 2 * 128), F32),
-            pltpu.VMEM((2, MEMBERS, MEMBERS), F32),
-            pltpu.VMEM((2, MEMBERS, MEMBERS), F32),
-            pltpu.VMEM((2, MEMBERS, MEMBERS), F32),
             pltpu.VMEM((MEMBERS, LANES), F32),
             pltpu.VMEM((2, 2, MEMBERS, MEMBERS), BF16),
+            *([pltpu.VMEM((MEMBERS, MEMBERS), BF16)] * 18),
         ],
         compiler_params=params(),
         name="analysis",
@@ -342,6 +351,9 @@
 def restore(cells):
     return pl.pallas_call(
         restore_kernel,
+        grid=(4,),
+        in_specs=[pl.BlockSpec((8, 1, 4 * PAIR), lambda y: (y, 0, 0))],
+        out_specs=pl.BlockSpec((LEVELS, 8, GY), lambda y: (0, 0, y)),
         out_shape=jax.ShapeDtypeStruct((LEVELS, 8, 4 * GY), F32),
         compiler_params=params(),
         name="restore",
@@ -358,8 +370,8 @@
     mixing, rate = prepare(blending_matrix, lateral_spreading)
     split = deal(ensemble.transpose(1, 0, 2))
     main = lax.all_to_all(split, "x", split_axis=0, concat_axis=0, tiled=True)
+    after = lax.ppermute(main[0], "zh", [((i + 1) % 4, i) for i in range(4)])
     before = lax.ppermute(main[3], "zh", [(i, (i + 1) % 4) for i in range(4)])
-    after = lax.ppermute(main[0], "zh", [((i + 1) % 4, i) for i in range(4)])
     inner, edges, mixed, rates, wide = forecast_interior(main, mixing, rate, obs_op)
     sent = forecast_edges(main, before, after, inner, edges, mixed, rates)
     owned = lax.all_to_all(sent, ("x", "y", "zl", "c"), split_axis=0, concat_axis=0, tiled=True)

time: 186 us -> 181 us (0.973)
  blocking collectives: 89.3 us -> 77.3 us
  waiting for transfers between devices: 25.6 us -> 34.3 us
    all_to_all x1, blocking collectives: 52.9 us -> 41 us  [shards(): lax.all_to_all(sent, ('x', 'y', 'zl', 'c'), split_axis=0, concat_axis=0,...]
    ppermute x1, starting transfers between devices: 17.4 us -> 5.56 us  [shards(): after = lax.ppermute(main[0], 'zh', [((i + 1) % 4, i) for i in range(4)])]
    ppermute x1, starting transfers between devices: 1.92 us -> 13.7 us  [shards(): before = lax.ppermute(main[3], 'zh', [(i, (i + 1) % 4) for i in range(4)])]
    ppermute x1, waiting for transfers between devices: 14.8 us -> 23.4 us  [shards(): after = lax.ppermute(main[0], 'zh', [((i + 1) % 4, i) for i in range(4)])]
where the time goes in v5:
time: 181 us; the launch traced here: 180 us
  blocking collectives  77.3 us (43%)
  Pallas kernels  42.5 us (23%)
  waiting for transfers between devices  34.3 us (19%)
  starting transfers between devices  24.2 us (13%)
  local copies, waits for them, and re-layouts  2.06 us (1%)
    all_to_all x1, blocking collectives, shards(): lax.all_to_all(sent, ('x', 'y', 'zl', 'c'), split_axis=0, concat_axis=0,...  41 us
    all_to_all x1, blocking collectives, shards(): lax.all_to_all(result, ('y', 'zl', 'c'), split_axis=0, concat_axis=0, til...  36.3 us
    pallas_call x1, Pallas kernels, analyse(): pl.pallas_call(analysis_kernel, out_shape=jax.ShapeDtypeStruct((32, 1, 4...  24.7 us
    ppermute x1, waiting for transfers between devices, shards(): after = lax.ppermute(main[0], 'zh', [((i + 1) % 4, i) for i in range(4)])  23.4 us
    ppermute x1, starting transfers between devices, shards(): before = lax.ppermute(main[3], 'zh', [(i, (i + 1) % 4) for i in range(4)])  13.7 us
    all_to_all x1, waiting for transfers between devices, shards(): main = lax.all_to_all(split, 'x', split_axis=0, concat_axis=0, tiled=True)  10.8 us
    pallas_call x1, Pallas kernels, forecast_interior(): pl.pallas_call(interior_kernel, out_shape=[jax.ShapeDtypeStruct((64, 1, P...  7.18 us
    ppermute x1, starting transfers between devices, shards(): after = lax.ppermute(main[0], 'zh', [((i + 1) % 4, i) for i in range(4)])  5.56 us
  transfers between devices with their start and end apart: 3, of which 2 were waited for; matrix products, arithmetic and copies ran while one was open for 0% of the time, Pallas kernels for 4%

profile of v5, /device:TPU:1, one launch (start us, length us, event | category | flops | bytes accessed | tf_op | source)
XLA Modules:
  0.0 180.4 jit_solution(14659303233729867005)
XLA Ops:
  0.0 1.3 copy-done
  1.3 1.3 deal.1
  2.6 5.0 %all-to-all-start = ((f32[4,76,2,512]{3,2,1,0:T(2,128)}), f32[4,76,2,512]{3,2,1,0:T(2,128)S(1)}, u32[]{:S(2)}, u32[]{:S(2)}) async-start(f32[4,76,2,512]{3,2,1,0:T(2,128)} %deal.1), calls=%async_computation | async-start | bytes 2490368 | tf_op jit(solution)/shard_map/all_to_all | solution.py:372
  7.6 0.0 copy-done.5
  7.6 0.1 copy.11.rate_ref
  7.7 0.0 copy-done.4
  7.7 0.1 copy.13
  7.8 0.1 copy.10.mix_ref
  7.9 0.0 copy-done.3
  7.9 0.2 copy.12.op_ref
  8.1 10.8 %all-to-all-done.main_ref = f32[4,76,2,512]{3,2,1,0:T(2,128)S(1)} async-done(((f32[4,76,2,512]{3,2,1,0:T(2,128)}), f32[4,76,2,512]{3,2,1,0:T(2,128)S(1)}, u32[]{:S(2)}, u32[]{:S(2)}) %all-to-all-start) | async-done | bytes 1245216 | tf_op jit(solution)/shard_map/all_to_all | solution.py:372
  18.9 0.2 slice_bitcast_fusion
  19.2 13.7 %collective-permute-start.1 = (f32[76,2,512]{2,1,0:T(2,128)S(1)}, f32[76,2,512]{2,1,0:T(2,128)S(1)}, u32[]{:S(2)}, u32[]{:S(2)}) collective-permute-start(f32[76,2,512]{2,1,0:T(2,128)S(1)} %get-tuple-element.15), channel_id=1, source_target_pairs={{0,4},{4,8},{8,12},{12,0},{1,5},{5,9},{9,13},{13,1},{2,6},{6,10},{... | collective-permute-start | bytes 933896 | tf_op jit(solution)/shard_map/ppermute | solution.py:374
  32.9 5.6 %collective-permute-start = (f32[76,2,512]{2,1,0:T(2,128)S(1)}, f32[76,2,512]{2,1,0:T(2,128)S(1)}, u32[]{:S(2)}, u32[]{:S(2)}) collective-permute-start(f32[76,2,512]{2,1,0:T(2,128)S(1)} %get-tuple-element.16), channel_id=1, source_target_pairs={{4,0},{8,4},{12,8},{0,12},{5,1},{9,5},{13,9},{1,13},{6,2},{10,6},{... | collective-permute-start | bytes 933896 | tf_op jit(solution)/shard_map/ppermute | solution.py:373
  38.5 7.2 %interior.1 = (f32[64,1,2432]{2,1,0:T(1,128)S(1)}, f32[3,2,4,80,128]{4,3,2,1,0:T(8,128)S(1)}, bf16[80,240]{1,0:T(8,128)(2,1)S(1)}, f32[80,128]{1,0:T(8,128)S(1)}, f32[256,1280]{1,0:T(8,128)S(1)}) custom-call(f32[4,76,2,512]{3,2,1,0:T(2,128)S(1)} %all-to-all-done.main_ref, f32[80,240]{1,0:T(8,128)S(1)} %copy.10.mix_ref, f32[80,1]{1,0:T(8,128)S(1)} %copy.11.rate_ref, ...), custom_call_target="tpu_custom_call" | custom-call | flops 10000000000 | bytes 8388608 | tf_op jit(solution)/shard_map/interior/pallas_call | solution.py:309
  45.6 0.0 collective-permute-done.1.prev_ref
  45.7 23.4 %collective-permute-done.next_ref = f32[76,2,512]{2,1,0:T(2,128)S(1)} collective-permute-done((f32[76,2,512]{2,1,0:T(2,128)S(1)}, f32[76,2,512]{2,1,0:T(2,128)S(1)}, u32[]{:S(2)}, u32[]{:S(2)}) %collective-permute-start) | collective-permute-done | bytes 311328 | tf_op jit(solution)/shard_map/ppermute | solution.py:373
  69.1 5.3 %edges.1 = f32[128,1,2432]{2,1,0:T(1,128)S(1)} custom-call(f32[4,76,2,512]{3,2,1,0:T(2,128)S(1)} %all-to-all-done.main_ref, f32[76,2,512]{2,1,0:T(2,128)S(1)} %collective-permute-done.next_ref, f32[76,2,512]{2,1,0:T(2,128)S(1)} %collective-permute-done.1.prev_ref, f32[64,1,2432]{2,1,0:T(1,128)S(1)} %get-tuple-element.10.inner_ref, ...), custom_call_target="tpu_custom_call" | custom-call | tf_op jit(solution)/shard_map/edges/pallas_call | solution.py:326
  74.4 0.0 copy-start.1
  74.4 0.0 copy-start.2
  74.4 41.0 %all_to_all.15.x_ref = f32[128,1,2432]{2,1,0:T(1,128)S(1)} all-to-all(f32[128,1,2432]{2,1,0:T(1,128)S(1)} %edges.1), channel_id=1, replica_groups=mesh['y'=4,'zl'=4,'c'=2,'zh'=4,'x'=4] {'x','y','zl','c'}, dimensions={0} | all-to-all | bytes 2490368 | tf_op jit(solution)/shard_map/all_to_all | solution.py:377
  115.4 24.7 %analysis.1 = f32[32,1,9728]{2,1,0:T(1,128)S(1)} custom-call(f32[128,1,2432]{2,1,0:T(1,128)S(1)} %all_to_all.15.x_ref, f32[256,1280]{1,0:T(8,128)S(1)} %get-tuple-element.14.wide, f32[2,128]{1,0:T(2,128)S(1)} %copy-done.1, f32[2,128]{1,0:T(2,128)S(1)} %copy-done.2), custom_call_target="tpu_custom_call" | custom-call | tf_op jit(solution)/shard_map/analysis/pallas_call | solution.py:336
  140.1 36.3 %all_to_all.16.in_ref = f32[32,1,9728]{2,1,0:T(1,128)S(1)} all-to-all(f32[32,1,9728]{2,1,0:T(1,128)S(1)} %analysis.1), channel_id=1, replica_groups=mesh['y'=4,'zl'=4,'c'=2,'zh'=4,'x'=4] {'y','zl','c'}, dimensions={0} | all-to-all | bytes 2490368 | tf_op jit(solution)/shard_map/all_to_all | solution.py:379
  176.4 4.0 %restore.1 = f32[76,8,512]{2,1,0:T(8,128)} custom-call(f32[32,1,9728]{2,1,0:T(1,128)S(1)} %all_to_all.16.in_ref), custom_call_target="tpu_custom_call" | custom-call | tf_op jit(solution)/shard_map/restore/pallas_call | solution.py:352
  (9 shorter events, 0.0 us)
Async XLA Ops:
  0.0 1.3 copy-start
  2.6 5.0 %copy-start.5 = (f32[76]{0:T(128)S(1)}, f32[76]{0:T(128)}, u32[]{:S(2)}) copy-start(f32[76]{0:T(128)} %param.8) | copy-start | bytes 916
  2.6 5.1 %copy-start.4 = (f32[76,76]{1,0:T(8,128)S(1)}, f32[76,76]{1,0:T(8,128)}, u32[]{:S(2)}) copy-start(f32[76,76]{1,0:T(8,128)} %param.7) | copy-start | bytes 69316
  2.6 5.3 %copy-start.3 = (f32[2,128,608]{1,2,0:T(8,128)S(1)}, f32[2,128,608]{1,2,0:T(8,128)}, u32[]{:S(2)}) copy-start(f32[2,128,608]{1,2,0:T(8,128)} %param.9) | copy-start | bytes 1867780
  2.6 16.4 %all-to-all-start = ((f32[4,76,2,512]{3,2,1,0:T(2,128)}), f32[4,76,2,512]{3,2,1,0:T(2,128)S(1)}, u32[]{:S(2)}, u32[]{:S(2)}) async-start(f32[4,76,2,512]{3,2,1,0:T(2,128)} %deal.1), calls=%async_computation | async-start | bytes 2490368 | tf_op jit(solution)/shard_map/all_to_all | solution.py:372
  19.2 26.5 %collective-permute-start.1 = (f32[76,2,512]{2,1,0:T(2,128)S(1)}, f32[76,2,512]{2,1,0:T(2,128)S(1)}, u32[]{:S(2)}, u32[]{:S(2)}) collective-permute-start(f32[76,2,512]{2,1,0:T(2,128)S(1)} %get-tuple-element.15), channel_id=1, source_target_pairs={{0,4},{4,8},{8,12},{12,0},{1,5},{5,9},{9,13},{13,1},{2,6},{6,10},{... | collective-permute-start | bytes 933896 | tf_op jit(solution)/shard_map/ppermute | solution.py:374
  32.9 36.2 %collective-permute-start = (f32[76,2,512]{2,1,0:T(2,128)S(1)}, f32[76,2,512]{2,1,0:T(2,128)S(1)}, u32[]{:S(2)}, u32[]{:S(2)}) collective-permute-start(f32[76,2,512]{2,1,0:T(2,128)S(1)} %get-tuple-element.16), channel_id=1, source_target_pairs={{4,0},{8,4},{12,8},{0,12},{5,1},{9,5},{13,9},{1,13},{6,2},{10,6},{... | collective-permute-start | bytes 933896 | tf_op jit(solution)/shard_map/ppermute | solution.py:373
  74.4 41.0 %copy-start.1 = (f32[2,128]{1,0:T(2,128)S(1)}, f32[2,128]{1,0:T(2,128)}, u32[]{:S(2)}) copy-start(f32[2,128]{1,0:T(2,128)} %obs_ref.1) | copy-start | bytes 3076
  74.4 41.0 %copy-start.2 = (f32[2,128]{1,0:T(2,128)S(1)}, f32[2,128]{1,0:T(2,128)}, u32[]{:S(2)}) copy-start(f32[2,128]{1,0:T(2,128)} %prec_ref.1) | copy-start | bytes 3076

commit v6 on v5

--- a/solution.py
+++ b/solution.py
@@ -35,21 +35,19 @@
     return high, mid, low
 
 
-def swap_blocks(x):
-    sub = lax.broadcasted_iota(jnp.int32, x.shape, 1)
-    block = lane_index(x.shape) // 16
-    for bit in (1, 2, 4):
-        up = (sub & bit) != 0
-        keep = up == ((block & bit) != 0)
-        lanes = 16 * bit
-        lower = pltpu.roll(pltpu.roll(x, 8 - bit, 1), lanes, 2)
-        if bit == 4:
-            other = lower
-        else:
-            upper = pltpu.roll(pltpu.roll(x, bit, 1), 128 - lanes, 2)
-            other = jnp.where(up, upper, lower)
-        x = jnp.where(keep, x, other)
-    return x
+def swap_blocks(tiles):
+    sub = lax.broadcasted_iota(jnp.int32, (8, 128), 0)
+    lane = lane_index((8, 128))
+    block, col = lane // 16, lane % 16
+    skew = ((block + sub) % 8) * 16 + col
+    turn = (sub - block) % 8
+    back = turn * 16 + col
+    result = []
+    for x in tiles:
+        for index, axis in ((skew, 1), (turn, 0), (back, 1)):
+            x = jnp.take_along_axis(x, index, axis=axis, mode="promise_in_bounds")
+        result.append(x)
+    return result
 
 
 def advance(window, mix_ref, rate_ref):
@@ -70,7 +68,7 @@
 def send_rows(results, row, out_ref):
     for i in range(2):
         both = jnp.concatenate([results[m][i][0:LEVELS] for m in range(2)], axis=0)
-        moved = swap_blocks(both.reshape(TILES, 8, GY))
+        moved = swap_blocks([both[tile * 8 : tile * 8 + 8] for tile in range(TILES)])
         for tile in range(TILES):
             out_ref[pl.ds((row + i) * 8, 8), 0, pl.ds(tile * 128, 128)] = moved[tile]
 
@@ -289,7 +287,8 @@
 def restore_kernel(in_ref, out_ref):
     for first in range(0, LEVELS, 19):
         tiles = [in_ref[:, 0, pl.ds((first + i) * 128, 128)] for i in range(19)]
-        out_ref[first : first + 19] = swap_blocks(jnp.stack(tiles, axis=0))
+        for i, moved in enumerate(swap_blocks(tiles)):
+            out_ref[first + i] = moved
 
 
 def params():

time: 181 us -> 179 us (0.989)
  Pallas kernels: 42.5 us -> 40.1 us
where the time goes in v6:
time: 179 us; the launch traced here: 178 us
  blocking collectives  77.3 us (43%)
  Pallas kernels  40.1 us (22%)
  waiting for transfers between devices  34.6 us (19%)
  starting transfers between devices  24.2 us (14%)
  local copies, waits for them, and re-layouts  2.06 us (1%)
    all_to_all x1, blocking collectives, shards(): lax.all_to_all(sent, ('x', 'y', 'zl', 'c'), split_axis=0, concat_axis=0,...  41 us
    all_to_all x1, blocking collectives, shards(): lax.all_to_all(result, ('y', 'zl', 'c'), split_axis=0, concat_axis=0, til...  36.3 us
    pallas_call x1, Pallas kernels, analyse(): pl.pallas_call(analysis_kernel, out_shape=jax.ShapeDtypeStruct((32, 1, 4...  24.7 us
    ppermute x1, waiting for transfers between devices, shards(): after = lax.ppermute(main[0], 'zh', [((i + 1) % 4, i) for i in range(4)])  23.8 us
    ppermute x1, starting transfers between devices, shards(): before = lax.ppermute(main[3], 'zh', [(i, (i + 1) % 4) for i in range(4)])  13.7 us
    all_to_all x1, waiting for transfers between devices, shards(): main = lax.all_to_all(split, 'x', split_axis=0, concat_axis=0, tiled=True)  10.8 us
    pallas_call x1, Pallas kernels, forecast_interior(): pl.pallas_call(interior_kernel, out_shape=[jax.ShapeDtypeStruct((64, 1, P...  6.8 us
    ppermute x1, starting transfers between devices, shards(): after = lax.ppermute(main[0], 'zh', [((i + 1) % 4, i) for i in range(4)])  5.56 us
  transfers between devices with their start and end apart: 3, of which 2 were waited for; matrix products, arithmetic and copies ran while one was open for 0% of the time, Pallas kernels for 4%

profile of v6, /device:TPU:1, one launch (start us, length us, event | category | flops | bytes accessed | tf_op | source)
XLA Modules:
  0.0 178.4 jit_solution(14388570095961177095)
XLA Ops:
  0.0 1.3 copy-done
  1.3 1.3 deal.1
  2.6 5.0 %all-to-all-start = ((f32[4,76,2,512]{3,2,1,0:T(2,128)}), f32[4,76,2,512]{3,2,1,0:T(2,128)S(1)}, u32[]{:S(2)}, u32[]{:S(2)}) async-start(f32[4,76,2,512]{3,2,1,0:T(2,128)} %deal.1), calls=%async_computation | async-start | bytes 2490368 | tf_op jit(solution)/shard_map/all_to_all | solution.py:371
  7.6 0.0 copy-done.5
  7.6 0.1 copy.11.rate_ref
  7.7 0.1 copy.13
  7.8 0.1 copy.10.mix_ref
  7.9 0.0 copy-done.3
  7.9 0.2 copy.12.op_ref
  8.1 10.8 %all-to-all-done.main_ref = f32[4,76,2,512]{3,2,1,0:T(2,128)S(1)} async-done(((f32[4,76,2,512]{3,2,1,0:T(2,128)}), f32[4,76,2,512]{3,2,1,0:T(2,128)S(1)}, u32[]{:S(2)}, u32[]{:S(2)}) %all-to-all-start) | async-done | bytes 1245216 | tf_op jit(solution)/shard_map/all_to_all | solution.py:371
  18.9 0.2 slice_bitcast_fusion
  19.2 13.7 %collective-permute-start.1 = (f32[76,2,512]{2,1,0:T(2,128)S(1)}, f32[76,2,512]{2,1,0:T(2,128)S(1)}, u32[]{:S(2)}, u32[]{:S(2)}) collective-permute-start(f32[76,2,512]{2,1,0:T(2,128)S(1)} %get-tuple-element.15), channel_id=1, source_target_pairs={{0,4},{4,8},{8,12},{12,0},{1,5},{5,9},{9,13},{13,1},{2,6},{6,10},{... | collective-permute-start | bytes 933896 | tf_op jit(solution)/shard_map/ppermute | solution.py:373
  32.9 5.6 %collective-permute-start = (f32[76,2,512]{2,1,0:T(2,128)S(1)}, f32[76,2,512]{2,1,0:T(2,128)S(1)}, u32[]{:S(2)}, u32[]{:S(2)}) collective-permute-start(f32[76,2,512]{2,1,0:T(2,128)S(1)} %get-tuple-element.16), channel_id=1, source_target_pairs={{4,0},{8,4},{12,8},{0,12},{5,1},{9,5},{13,9},{1,13},{6,2},{10,6},{... | collective-permute-start | bytes 933896 | tf_op jit(solution)/shard_map/ppermute | solution.py:372
  38.5 6.8 %interior.1 = (f32[64,1,2432]{2,1,0:T(1,128)S(1)}, f32[3,2,4,80,128]{4,3,2,1,0:T(8,128)S(1)}, bf16[80,240]{1,0:T(8,128)(2,1)S(1)}, f32[80,128]{1,0:T(8,128)S(1)}, f32[256,1280]{1,0:T(8,128)S(1)}) custom-call(f32[4,76,2,512]{3,2,1,0:T(2,128)S(1)} %all-to-all-done.main_ref, f32[80,240]{1,0:T(8,128)S(1)} %copy.10.mix_ref, f32[80,1]{1,0:T(8,128)S(1)} %copy.11.rate_ref, ...), custom_call_target="tpu_custom_call" | custom-call | flops 10000000000 | bytes 8388608 | tf_op jit(solution)/shard_map/interior/pallas_call | solution.py:308
  45.3 0.0 collective-permute-done.1.prev_ref
  45.3 23.8 %collective-permute-done.next_ref = f32[76,2,512]{2,1,0:T(2,128)S(1)} collective-permute-done((f32[76,2,512]{2,1,0:T(2,128)S(1)}, f32[76,2,512]{2,1,0:T(2,128)S(1)}, u32[]{:S(2)}, u32[]{:S(2)}) %collective-permute-start) | collective-permute-done | bytes 311328 | tf_op jit(solution)/shard_map/ppermute | solution.py:372
  69.1 4.9 %edges.1 = f32[128,1,2432]{2,1,0:T(1,128)S(1)} custom-call(f32[4,76,2,512]{3,2,1,0:T(2,128)S(1)} %all-to-all-done.main_ref, f32[76,2,512]{2,1,0:T(2,128)S(1)} %collective-permute-done.next_ref, f32[76,2,512]{2,1,0:T(2,128)S(1)} %collective-permute-done.1.prev_ref, f32[64,1,2432]{2,1,0:T(1,128)S(1)} %get-tuple-element.10.inner_ref, ...), custom_call_target="tpu_custom_call" | custom-call | tf_op jit(solution)/shard_map/edges/pallas_call | solution.py:325
  74.0 0.0 copy-start.1
  74.0 0.0 copy-start.2
  74.1 41.0 %all_to_all.15.x_ref = f32[128,1,2432]{2,1,0:T(1,128)S(1)} all-to-all(f32[128,1,2432]{2,1,0:T(1,128)S(1)} %edges.1), channel_id=1, replica_groups=mesh['y'=4,'zl'=4,'c'=2,'zh'=4,'x'=4] {'x','y','zl','c'}, dimensions={0} | all-to-all | bytes 2490368 | tf_op jit(solution)/shard_map/all_to_all | solution.py:376
  115.0 0.0 copy-done.1
  115.0 24.7 %analysis.1 = f32[32,1,9728]{2,1,0:T(1,128)S(1)} custom-call(f32[128,1,2432]{2,1,0:T(1,128)S(1)} %all_to_all.15.x_ref, f32[256,1280]{1,0:T(8,128)S(1)} %get-tuple-element.14.wide, f32[2,128]{1,0:T(2,128)S(1)} %copy-done.1, f32[2,128]{1,0:T(2,128)S(1)} %copy-done.2), custom_call_target="tpu_custom_call" | custom-call | tf_op jit(solution)/shard_map/analysis/pallas_call | solution.py:335
  139.7 36.3 %all_to_all.16.in_ref = f32[32,1,9728]{2,1,0:T(1,128)S(1)} all-to-all(f32[32,1,9728]{2,1,0:T(1,128)S(1)} %analysis.1), channel_id=1, replica_groups=mesh['y'=4,'zl'=4,'c'=2,'zh'=4,'x'=4] {'y','zl','c'}, dimensions={0} | all-to-all | bytes 2490368 | tf_op jit(solution)/shard_map/all_to_all | solution.py:378
  176.0 2.4 %restore.1 = f32[76,8,512]{2,1,0:T(8,128)} custom-call(f32[32,1,9728]{2,1,0:T(1,128)S(1)} %all_to_all.16.in_ref), custom_call_target="tpu_custom_call" | custom-call | tf_op jit(solution)/shard_map/restore/pallas_call | solution.py:351
  (9 shorter events, 0.0 us)
Async XLA Ops:
  0.0 1.3 copy-start
  2.6 5.0 %copy-start.5 = (f32[76]{0:T(128)S(1)}, f32[76]{0:T(128)}, u32[]{:S(2)}) copy-start(f32[76]{0:T(128)} %param.8) | copy-start | bytes 916
  2.6 5.1 %copy-start.4 = (f32[76,76]{1,0:T(8,128)S(1)}, f32[76,76]{1,0:T(8,128)}, u32[]{:S(2)}) copy-start(f32[76,76]{1,0:T(8,128)} %param.7) | copy-start | bytes 69316
  2.6 5.3 %copy-start.3 = (f32[2,128,608]{1,2,0:T(8,128)S(1)}, f32[2,128,608]{1,2,0:T(8,128)}, u32[]{:S(2)}) copy-start(f32[2,128,608]{1,2,0:T(8,128)} %param.9) | copy-start | bytes 1867780
  2.6 16.4 %all-to-all-start = ((f32[4,76,2,512]{3,2,1,0:T(2,128)}), f32[4,76,2,512]{3,2,1,0:T(2,128)S(1)}, u32[]{:S(2)}, u32[]{:S(2)}) async-start(f32[4,76,2,512]{3,2,1,0:T(2,128)} %deal.1), calls=%async_computation | async-start | bytes 2490368 | tf_op jit(solution)/shard_map/all_to_all | solution.py:371
  19.2 26.1 %collective-permute-start.1 = (f32[76,2,512]{2,1,0:T(2,128)S(1)}, f32[76,2,512]{2,1,0:T(2,128)S(1)}, u32[]{:S(2)}, u32[]{:S(2)}) collective-permute-start(f32[76,2,512]{2,1,0:T(2,128)S(1)} %get-tuple-element.15), channel_id=1, source_target_pairs={{0,4},{4,8},{8,12},{12,0},{1,5},{5,9},{9,13},{13,1},{2,6},{6,10},{... | collective-permute-start | bytes 933896 | tf_op jit(solution)/shard_map/ppermute | solution.py:373
  32.9 36.2 %collective-permute-start = (f32[76,2,512]{2,1,0:T(2,128)S(1)}, f32[76,2,512]{2,1,0:T(2,128)S(1)}, u32[]{:S(2)}, u32[]{:S(2)}) collective-permute-start(f32[76,2,512]{2,1,0:T(2,128)S(1)} %get-tuple-element.16), channel_id=1, source_target_pairs={{4,0},{8,4},{12,8},{0,12},{5,1},{9,5},{13,9},{1,13},{6,2},{10,6},{... | collective-permute-start | bytes 933896 | tf_op jit(solution)/shard_map/ppermute | solution.py:372
  74.0 41.0 %copy-start.1 = (f32[2,128]{1,0:T(2,128)S(1)}, f32[2,128]{1,0:T(2,128)}, u32[]{:S(2)}) copy-start(f32[2,128]{1,0:T(2,128)} %obs_ref.1) | copy-start | bytes 3076
  74.0 41.0 %copy-start.2 = (f32[2,128]{1,0:T(2,128)S(1)}, f32[2,128]{1,0:T(2,128)}, u32[]{:S(2)}) copy-start(f32[2,128]{1,0:T(2,128)} %prec_ref.1) | copy-start | bytes 3076

commit v7 on v6

--- a/solution.py
+++ b/solution.py
@@ -126,10 +126,10 @@
             width = 128 if block < 4 else 608 - 512
             piece = split3(op_ref[j, :, pl.ds(block * 128, width)])
             grown = [jnp.dot(p, spread[0:width], preferred_element_type=F32) for p in piece]
-            full = (grown[0] + grown[1]) + grown[2]
-            wide_ref[j * 128 : (j + 1) * 128, block * 256 : (block + 1) * 256] = jnp.where(
-                group == j, full, 0.0
-            )
+            for i in range(3):
+                wide_ref[i, j * 128 : (j + 1) * 128, block * 256 : (block + 1) * 256] = jnp.where(
+                    group == j, grown[i], 0.0
+                ).astype(BF16)
 
 
 def edge_kernel(main_ref, next_ref, prev_ref, inner_ref, edge_ref, mix_ref, rate_ref, out_ref, state, sem):
@@ -186,11 +186,16 @@
         lanes = pl.ds(tile * 128, 128)
         pert[0:rows, lanes] = even - mean
         pert[rows : 2 * rows, lanes] = odd - mean
-        pert[2 * rows : 2 * rows + 8, lanes] = jnp.broadcast_to(mean, (8, 128))
-
-    yref[...] = lax.dot_general(
-        pert[...], wide[...], (((1,), (1,)), ((), ())), precision=HIGHEST, preferred_element_type=F32
-    )
+        pert[2 * rows : 2 * rows + 16, lanes] = jnp.broadcast_to(mean, (16, 128))
+
+    pieces = split3(pert[...])
+    sums = None
+    for i, k in ((2, 0), (0, 2), (1, 1), (1, 0), (0, 1), (0, 0)):
+        term = lax.dot_general(
+            pieces[i], wide[k], (((1,), (1,)), ((), ())), preferred_element_type=F32
+        )
+        sums = term if sums is None else term + sums
+    yref[...] = sums
     eye = jnp.where(
         lax.broadcasted_iota(jnp.int32, (MEMBERS, MEMBERS), 0) == lane_index((MEMBERS, MEMBERS)), 1.0, 0.0
     )
@@ -312,7 +317,7 @@
             jax.ShapeDtypeStruct((NSTEP - 1, 2, 4, PADDED, GY), F32),
             jax.ShapeDtypeStruct((PADDED, 3 * PADDED), BF16),
             jax.ShapeDtypeStruct((PADDED, GY), F32),
-            jax.ShapeDtypeStruct((2 * 128, LANES), F32),
+            jax.ShapeDtypeStruct((3, 2 * 128, LANES), BF16),
         ],
         scratch_shapes=[pltpu.VMEM((2, 2, 16, PADDED, GY), F32)],
         compiler_params=params(),
@@ -336,8 +341,8 @@
         analysis_kernel,
         out_shape=jax.ShapeDtypeStruct((32, 1, 4 * PAIR), F32),
         scratch_shapes=[
-            pltpu.VMEM((MEMBERS + 8, LANES), F32),
-            pltpu.VMEM((MEMBERS + 8, 2 * 128), F32),
+            pltpu.VMEM((MEMBERS + 16, LANES), F32),
+            pltpu.VMEM((MEMBERS + 16, 2 * 128), F32),
             pltpu.VMEM((MEMBERS, LANES), F32),
             pltpu.VMEM((2, 2, MEMBERS, MEMBERS), BF16),
             *([pltpu.VMEM((MEMBERS, MEMBERS), BF16)] * 18),

time: 179 us -> 179 us (level)
  no operation moved by 1% of the time
where the time goes in v7:
time: 179 us
  blocking collectives  77.3 us (43%)
  Pallas kernels  40.4 us (23%)
  waiting for transfers between devices  34.6 us (19%)
  starting transfers between devices  24.2 us (14%)
  local copies, waits for them, and re-layouts  2.06 us (1%)
    all_to_all x1, blocking collectives, shards(): lax.all_to_all(sent, ('x', 'y', 'zl', 'c'), split_axis=0, concat_axis=0,...  41 us
    all_to_all x1, blocking collectives, shards(): lax.all_to_all(result, ('y', 'zl', 'c'), split_axis=0, concat_axis=0, til...  36.3 us
    pallas_call x1, Pallas kernels, analyse(): pl.pallas_call(analysis_kernel, out_shape=jax.ShapeDtypeStruct((32, 1, 4...  25 us
    ppermute x1, waiting for transfers between devices, shards(): after = lax.ppermute(main[0], 'zh', [((i + 1) % 4, i) for i in range(4)])  23.8 us
    ppermute x1, starting transfers between devices, shards(): before = lax.ppermute(main[3], 'zh', [(i, (i + 1) % 4) for i in range(4)])  13.7 us
    all_to_all x1, waiting for transfers between devices, shards(): main = lax.all_to_all(split, 'x', split_axis=0, concat_axis=0, tiled=True)  10.8 us
    pallas_call x1, Pallas kernels, forecast_interior(): pl.pallas_call(interior_kernel, out_shape=[jax.ShapeDtypeStruct((64, 1, P...  6.8 us
    ppermute x1, starting transfers between devices, shards(): after = lax.ppermute(main[0], 'zh', [((i + 1) % 4, i) for i in range(4)])  5.56 us
  transfers between devices with their start and end apart: 3, of which 2 were waited for; matrix products, arithmetic and copies ran while one was open for 0% of the time, Pallas kernels for 4%

profile of v7, /device:TPU:1, one launch (start us, length us, event | category | flops | bytes accessed | tf_op | source)
XLA Modules:
  0.0 178.8 jit_solution(2939843363841010606)
XLA Ops:
  0.0 1.3 copy-done
  1.3 1.3 deal.1
  2.6 5.0 %all-to-all-start = ((f32[4,76,2,512]{3,2,1,0:T(2,128)}), f32[4,76,2,512]{3,2,1,0:T(2,128)S(1)}, u32[]{:S(2)}, u32[]{:S(2)}) async-start(f32[4,76,2,512]{3,2,1,0:T(2,128)} %deal.1), calls=%async_computation | async-start | bytes 2490368 | tf_op jit(solution)/shard_map/all_to_all | solution.py:376
  7.6 0.0 copy-done.5
  7.6 0.1 copy.11.rate_ref
  7.7 0.1 copy.13
  7.8 0.1 copy.10.mix_ref
  7.9 0.0 copy-done.3
  7.9 0.2 copy.12.op_ref
  8.1 10.8 %all-to-all-done.main_ref = f32[4,76,2,512]{3,2,1,0:T(2,128)S(1)} async-done(((f32[4,76,2,512]{3,2,1,0:T(2,128)}), f32[4,76,2,512]{3,2,1,0:T(2,128)S(1)}, u32[]{:S(2)}, u32[]{:S(2)}) %all-to-all-start) | async-done | bytes 1245216 | tf_op jit(solution)/shard_map/all_to_all | solution.py:376
  18.9 0.2 slice_bitcast_fusion
  19.2 13.7 %collective-permute-start.1 = (f32[76,2,512]{2,1,0:T(2,128)S(1)}, f32[76,2,512]{2,1,0:T(2,128)S(1)}, u32[]{:S(2)}, u32[]{:S(2)}) collective-permute-start(f32[76,2,512]{2,1,0:T(2,128)S(1)} %get-tuple-element.15), channel_id=1, source_target_pairs={{0,4},{4,8},{8,12},{12,0},{1,5},{5,9},{9,13},{13,1},{2,6},{6,10},{... | collective-permute-start | bytes 933896 | tf_op jit(solution)/shard_map/ppermute | solution.py:378
  32.9 5.6 %collective-permute-start = (f32[76,2,512]{2,1,0:T(2,128)S(1)}, f32[76,2,512]{2,1,0:T(2,128)S(1)}, u32[]{:S(2)}, u32[]{:S(2)}) collective-permute-start(f32[76,2,512]{2,1,0:T(2,128)S(1)} %get-tuple-element.16), channel_id=1, source_target_pairs={{4,0},{8,4},{12,8},{0,12},{5,1},{9,5},{13,9},{1,13},{6,2},{10,6},{... | collective-permute-start | bytes 933896 | tf_op jit(solution)/shard_map/ppermute | solution.py:377
  38.5 6.8 %interior.1 = (f32[64,1,2432]{2,1,0:T(1,128)S(1)}, f32[3,2,4,80,128]{4,3,2,1,0:T(8,128)S(1)}, bf16[80,240]{1,0:T(8,128)(2,1)S(1)}, f32[80,128]{1,0:T(8,128)S(1)}, bf16[3,256,1280]{2,1,0:T(8,128)(2,1)S(1)}) custom-call(f32[4,76,2,512]{3,2,1,0:T(2,128)S(1)} %all-to-all-done.main_ref, f32[80,240]{1,0:T(8,128)S(1)} %copy.10.mix_ref, f32[80,1]{1,0:T(8,128)S(1)} %copy.11.rate_ref, ...), custom_call_target="tpu_custom_call" | custom-call | flops 10000000000 | bytes 8388608 | tf_op jit(solution)/shard_map/interior/pallas_call | solution.py:313
  45.3 0.0 collective-permute-done.1.prev_ref
  45.3 23.8 %collective-permute-done.next_ref = f32[76,2,512]{2,1,0:T(2,128)S(1)} collective-permute-done((f32[76,2,512]{2,1,0:T(2,128)S(1)}, f32[76,2,512]{2,1,0:T(2,128)S(1)}, u32[]{:S(2)}, u32[]{:S(2)}) %collective-permute-start) | collective-permute-done | bytes 311328 | tf_op jit(solution)/shard_map/ppermute | solution.py:377
  69.1 4.9 %edges.1 = f32[128,1,2432]{2,1,0:T(1,128)S(1)} custom-call(f32[4,76,2,512]{3,2,1,0:T(2,128)S(1)} %all-to-all-done.main_ref, f32[76,2,512]{2,1,0:T(2,128)S(1)} %collective-permute-done.next_ref, f32[76,2,512]{2,1,0:T(2,128)S(1)} %collective-permute-done.1.prev_ref, f32[64,1,2432]{2,1,0:T(1,128)S(1)} %get-tuple-element.10.inner_ref, ...), custom_call_target="tpu_custom_call" | custom-call | tf_op jit(solution)/shard_map/edges/pallas_call | solution.py:330
  74.0 0.0 copy-start.1
  74.0 0.0 copy-start.2
  74.1 41.0 %all_to_all.15.x_ref = f32[128,1,2432]{2,1,0:T(1,128)S(1)} all-to-all(f32[128,1,2432]{2,1,0:T(1,128)S(1)} %edges.1), channel_id=1, replica_groups=mesh['y'=4,'zl'=4,'c'=2,'zh'=4,'x'=4] {'x','y','zl','c'}, dimensions={0} | all-to-all | bytes 2490368 | tf_op jit(solution)/shard_map/all_to_all | solution.py:381
  115.0 0.0 copy-done.1
  115.0 25.0 %analysis.1 = f32[32,1,9728]{2,1,0:T(1,128)S(1)} custom-call(f32[128,1,2432]{2,1,0:T(1,128)S(1)} %all_to_all.15.x_ref, bf16[3,256,1280]{2,1,0:T(8,128)(2,1)S(1)} %get-tuple-element.14.wide, f32[2,128]{1,0:T(2,128)S(1)} %copy-done.1, f32[2,128]{1,0:T(2,128)S(1)} %copy-done.2), custom_call_target="tpu_custom_call" | custom-call | tf_op jit(solution)/shard_map/analysis/pallas_call | solution.py:340
  140.0 36.3 %all_to_all.16.in_ref = f32[32,1,9728]{2,1,0:T(1,128)S(1)} all-to-all(f32[32,1,9728]{2,1,0:T(1,128)S(1)} %analysis.1), channel_id=1, replica_groups=mesh['y'=4,'zl'=4,'c'=2,'zh'=4,'x'=4] {'y','zl','c'}, dimensions={0} | all-to-all | bytes 2490368 | tf_op jit(solution)/shard_map/all_to_all | solution.py:383
  176.4 2.4 %restore.1 = f32[76,8,512]{2,1,0:T(8,128)} custom-call(f32[32,1,9728]{2,1,0:T(1,128)S(1)} %all_to_all.16.in_ref), custom_call_target="tpu_custom_call" | custom-call | tf_op jit(solution)/shard_map/restore/pallas_call | solution.py:356
  (9 shorter events, 0.0 us)
Async XLA Ops:
  0.0 1.3 copy-start
  2.6 5.0 %copy-start.5 = (f32[76]{0:T(128)S(1)}, f32[76]{0:T(128)}, u32[]{:S(2)}) copy-start(f32[76]{0:T(128)} %param.8) | copy-start | bytes 916
  2.6 5.1 %copy-start.4 = (f32[76,76]{1,0:T(8,128)S(1)}, f32[76,76]{1,0:T(8,128)}, u32[]{:S(2)}) copy-start(f32[76,76]{1,0:T(8,128)} %param.7) | copy-start | bytes 69316
  2.6 5.3 %copy-start.3 = (f32[2,128,608]{1,2,0:T(8,128)S(1)}, f32[2,128,608]{1,2,0:T(8,128)}, u32[]{:S(2)}) copy-start(f32[2,128,608]{1,2,0:T(8,128)} %param.9) | copy-start | bytes 1867780
  2.6 16.4 %all-to-all-start = ((f32[4,76,2,512]{3,2,1,0:T(2,128)}), f32[4,76,2,512]{3,2,1,0:T(2,128)S(1)}, u32[]{:S(2)}, u32[]{:S(2)}) async-start(f32[4,76,2,512]{3,2,1,0:T(2,128)} %deal.1), calls=%async_computation | async-start | bytes 2490368 | tf_op jit(solution)/shard_map/all_to_all | solution.py:376
  19.2 26.1 %collective-permute-start.1 = (f32[76,2,512]{2,1,0:T(2,128)S(1)}, f32[76,2,512]{2,1,0:T(2,128)S(1)}, u32[]{:S(2)}, u32[]{:S(2)}) collective-permute-start(f32[76,2,512]{2,1,0:T(2,128)S(1)} %get-tuple-element.15), channel_id=1, source_target_pairs={{0,4},{4,8},{8,12},{12,0},{1,5},{5,9},{9,13},{13,1},{2,6},{6,10},{... | collective-permute-start | bytes 933896 | tf_op jit(solution)/shard_map/ppermute | solution.py:378
  32.9 36.2 %collective-permute-start = (f32[76,2,512]{2,1,0:T(2,128)S(1)}, f32[76,2,512]{2,1,0:T(2,128)S(1)}, u32[]{:S(2)}, u32[]{:S(2)}) collective-permute-start(f32[76,2,512]{2,1,0:T(2,128)S(1)} %get-tuple-element.16), channel_id=1, source_target_pairs={{4,0},{8,4},{12,8},{0,12},{5,1},{9,5},{13,9},{1,13},{6,2},{10,6},{... | collective-permute-start | bytes 933896 | tf_op jit(solution)/shard_map/ppermute | solution.py:377
  74.0 41.0 %copy-start.1 = (f32[2,128]{1,0:T(2,128)S(1)}, f32[2,128]{1,0:T(2,128)}, u32[]{:S(2)}) copy-start(f32[2,128]{1,0:T(2,128)} %obs_ref.1) | copy-start | bytes 3076
  74.0 41.0 %copy-start.2 = (f32[2,128]{1,0:T(2,128)S(1)}, f32[2,128]{1,0:T(2,128)}, u32[]{:S(2)}) copy-start(f32[2,128]{1,0:T(2,128)} %prec_ref.1) | copy-start | bytes 3076
